TPU v7x, 512 devices: a whole 4x8x8 slice. The times are simulated.
512 devices in a mesh: pair: 32 (over x, z_lo, core), row: 2 (over z_hi), col: 8 (over y).
Axes of the slice: x: 4, y: 8, z: 8 (z_hi: 2, z_lo: 4; z = z_hi * 4 + z_lo), core: 2. Of those that a mesh axis runs over, the one named last changes fastest.
Arguments:
- limbs: int32 [6, 16384, 2048], P(None, 'pair', ('row', 'col')), parts along dimension 1, may hold values from 0 to 65535
Outputs:
- products: float32 [3, 16384, 2048], P(None, 'pair', ('row', 'col')), parts along dimension 1
There are 32 independent parts, one for each index of `pair`. A program takes and returns all parts, laid end to end along the dimension named above; each array names one. Nothing has to cross between parts.
All inputs are finite; a program needn't handle non-finite values.
Results may differ from a plain program's by a relative error of at most 0.00007.
Values sent between devices are 32-bit elements; how exact they have to be, the bound alone decides.
No kernel may reach another device: no remote copies, remote signals or barrier semaphores. Data moves between devices by JAX's collectives and lax.ppermute only.
A program may use at most 64 MiB of HBM per device.

v0:
```python
import math

import jax
import jax.numpy as jnp
from jax import lax
from jax.sharding import PartitionSpec as P

highest = lax.Precision.HIGHEST


def phases(multiple, period):
    angles = multiple.astype(jnp.float32) * (math.pi / period)
    return (jnp.cos(angles), -jnp.sin(angles))


def dft_table(length):
    indices = jnp.arange(length, dtype=jnp.int32)
    return phases(2 * (indices[:, None] * indices[None, :] % length), length)


def mixing(former, latter, formula):
    return jnp.einsum(formula, former, latter, precision=highest)


def multiply_pair(ar, ai, br, bi):
    return ar * br - ai * bi, ar * bi + ai * br


def body(limbs):
    groups = lax.axis_size(("row", "col"))
    number, height, narrow = limbs.shape
    breadth = narrow * groups
    limb_total = height * breadth
    half = height // 2
    local = half // groups
    device = lax.axis_index(("row", "col"))
    balanced = (limbs - 32768).astype(jnp.float32) / 32768.0

    half_index = jnp.arange(half, dtype=jnp.int32)
    row_index = jnp.arange(height, dtype=jnp.int32)
    row_cos, row_sin = phases(
        row_index[None, :] * (2 * half_index[:, None] + 1) % (2 * height), height
    )
    columns = device * narrow + jnp.arange(narrow, dtype=jnp.int32)
    turn_cos, turn_sin = phases(
        columns[None, :] * (2 * half_index[:, None] + 1) % (2 * limb_total), limb_total
    )

    real_rows = mixing(row_cos, balanced, "ja,iab->ijb")
    imag_rows = mixing(row_sin, balanced, "ja,iab->ijb")
    turned = jnp.stack(
        (
            real_rows * turn_cos - imag_rows * turn_sin,
            real_rows * turn_sin + imag_rows * turn_cos,
        )
    )
    send = turned.reshape(2, number, groups, local, narrow).transpose(2, 0, 1, 3, 4)
    received = lax.all_to_all(send, ("row", "col"), 0, 0, tiled=True)

    outer_cos, outer_sin = dft_table(groups)
    forward_block = jnp.stack(
        (
            jnp.stack((outer_cos, -outer_sin), -1),
            jnp.stack((outer_sin, outer_cos), -1),
        ),
        1,
    ).reshape(2 * groups, 2 * groups)
    mixed = jnp.dot(
        forward_block, received.reshape(2 * groups, -1), precision=highest
    ).reshape(groups, 2, number, local, narrow)
    outer_index = jnp.arange(groups, dtype=jnp.int32)
    inner_index = jnp.arange(narrow, dtype=jnp.int32)
    twist_cos, twist_sin = phases(
        2 * (outer_index[:, None] * inner_index[None, :] % breadth), breadth
    )
    twist_cos = twist_cos[:, None, None, :]
    twist_sin = twist_sin[:, None, None, :]
    mixed_re = mixed[:, 0]
    mixed_im = mixed[:, 1]
    turned_re = mixed_re * twist_cos - mixed_im * twist_sin
    turned_im = mixed_re * twist_sin + mixed_im * twist_cos
    inner_cos, inner_sin = dft_table(narrow)
    spec_re = mixing(turned_re, inner_cos, "kijq,qm->kijm") - mixing(
        turned_im, inner_sin, "kijq,qm->kijm"
    )
    spec_im = mixing(turned_re, inner_sin, "kijq,qm->kijm") + mixing(
        turned_im, inner_cos, "kijq,qm->kijm"
    )

    def spectrum(k):
        return spec_re[:, k], spec_im[:, k]

    first = multiply_pair(*spectrum(0), *spectrum(3))
    second = multiply_pair(*spectrum(1), *spectrum(4))
    third_a = multiply_pair(*spectrum(2), *spectrum(4))
    third_b = multiply_pair(*spectrum(0), *spectrum(5))
    comb_re = jnp.stack((first[0], second[0], third_a[0] + third_b[0]), axis=1)
    comb_im = jnp.stack((first[1], second[1], third_a[1] + third_b[1]), axis=1)

    back_re = mixing(comb_re, inner_cos, "kijm,qm->kijq") + mixing(
        comb_im, inner_sin, "kijm,qm->kijq"
    )
    back_im = mixing(comb_im, inner_cos, "kijm,qm->kijq") - mixing(
        comb_re, inner_sin, "kijm,qm->kijq"
    )
    untwist_re = back_re * twist_cos + back_im * twist_sin
    untwist_im = back_im * twist_cos - back_re * twist_sin
    inverse_block = jnp.stack(
        (
            jnp.stack((outer_cos, outer_sin), -1),
            jnp.stack((-outer_sin, outer_cos), -1),
        ),
        1,
    ).reshape(2 * groups, 2 * groups)
    outgoing = jnp.dot(
        inverse_block,
        jnp.stack((untwist_re, untwist_im), axis=1).reshape(2 * groups, -1),
        precision=highest,
    ).reshape(groups, 2, 3, local, narrow)
    pieces = lax.all_to_all(outgoing, ("row", "col"), 0, 0, tiled=True)

    turn_cos = turn_cos.reshape(groups, 1, local, narrow)
    turn_sin = turn_sin.reshape(groups, 1, local, narrow)
    real_part = pieces[:, 0] * turn_cos + pieces[:, 1] * turn_sin
    imag_part = pieces[:, 1] * turn_cos - pieces[:, 0] * turn_sin
    scale_factor = 2.0 / (limb_total * math.sqrt(limb_total))
    row_cos = row_cos.reshape(groups, local, height)
    row_sin = row_sin.reshape(groups, local, height)
    total = mixing(row_cos, real_part, "sja,sijb->iab") + mixing(
        row_sin, imag_part, "sja,sijb->iab"
    )
    return total * scale_factor


def solution(mesh):
    in_specs = (P(None, "pair", ("row", "col")),)
    out_specs = P(None, "pair", ("row", "col"))
    return jax.shard_map(body, mesh=mesh, in_specs=in_specs, out_specs=out_specs, check_vma=False)
```

profile of v0, /device:TPU:8, one launch (start us, length us, event | category | flops | bytes accessed | tf_op | source)
XLA Modules:
  0.0 128.5 jit_solution(12396871702589647053)
XLA Ops:
  0.0 0.6 fusion.77
  0.6 6.1 %fusion.5 = f32[6,256,128]{1,2,0:T(8,128)S(1)} fusion(s32[6,512,128]{2,1,0:T(8,128)} %param.1, s32[256]{0:T(256)S(1)} %multiply_add_fusion.5), kind=kOutput, calls=%fused_computation.7 | convolution fusion | flops 1210974208 | bytes 2360320 | tf_op jit(solution)/shard_map/ja,iab->ijb/dot_general | solution.py:22
  6.7 4.7 %multiply_subtract_fusion.1 = (f32[6,256,128]{1,2,0:T(8,128)S(1)}, f32[6,256,128]{1,2,0:T(8,128)S(1)}) fusion(f32[6,256,128]{1,2,0:T(8,128)S(1)} %fusion.5, f32[256,128]{0,1:T(8,128)S(1)} %get-tuple-element.28, f32[256,128]{0,1:T(8,128)S(1)} %get-tuple-element.27, s32[256]{0:T(256)S(1)} %multiply_add_fusion.5, s32[6,512,128]{2,1,0:T(8,128)S(1)} %copy-done), kind=kOutput, calls=%fused_computation.30 | convolution fusion | flops 1212284928 | bytes 4195328 | tf_op jit(solution)/shard_map/ja,iab->ijb/dot_general | solution.py:22
  12.1 1.4 %copy.34 = f32[16,2,6,16,128]{4,3,2,1,0:T(8,128)} copy(f32[16,2,6,16,128]{4,3,0,2,1:T(8,128)S(1)} %maximum_bitcast_fusion) | data formatting | bytes 3145728 | tf_op jit(solution)/shard_map/transpose | solution.py:57
  13.5 16.0 %all-to-all-start = ((f32[16,2,6,16,128]{4,3,2,1,0:T(8,128)}), f32[16,2,6,16,128]{4,3,2,1,0:T(8,128)S(1)}, u32[]{:S(2)}, u32[]{:S(2)}) async-start(f32[16,2,6,16,128]{4,3,2,1,0:T(8,128)} %copy.34), calls=%async_computation | async-start | bytes 3145728 | tf_op jit(solution)/shard_map/all_to_all | solution.py:58
  30.4 44.9 %all-to-all-done = f32[16,2,6,16,128]{4,3,2,1,0:T(8,128)S(1)} async-done(((f32[16,2,6,16,128]{4,3,2,1,0:T(8,128)}), f32[16,2,6,16,128]{4,3,2,1,0:T(8,128)S(1)}, u32[]{:S(2)}, u32[]{:S(2)}) %all-to-all-start) | async-done | bytes 1572896 | tf_op jit(solution)/shard_map/all_to_all | solution.py:58
  75.8 2.3 %fusion = f32[16,2,6,16,128]{4,0,3,2,1:T(8,128)S(1)} fusion(f32[6,16,128,32]{2,1,0,3:T(8,128)S(1)} %bitcast.126, f32[16,1,32]{2,0,1:T(8,128)S(1)} %copy.29, f32[16,1,32]{2,0,1:T(8,128)S(1)} %copy.28), kind=kOutput, calls=%fused_computation.1 | convolution fusion | flops 150995968 | bytes 3149824 | tf_op jit(solution)/shard_map/dot_general | solution.py:68
  78.3 1.2 fusion.21
  79.5 1.2 fusion.19
  80.7 1.2 convolution_subtract_fusion
  81.9 1.2 convolution_add_fusion
  83.3 0.7 fusion.49
  84.0 0.7 fusion.48
  84.7 0.7 convolution_subtract_fusion.1
  85.4 0.8 add_bitcast_fusion
  86.9 0.9 fusion.10
  87.8 1.1 copy.42
  88.9 12.2 %all-to-all-start.1 = ((f32[16,2,3,16,128]{4,3,2,1,0:T(8,128)}), f32[16,2,3,16,128]{4,3,2,1,0:T(8,128)S(1)}, u32[]{:S(2)}, u32[]{:S(2)}) async-start(f32[16,2,3,16,128]{4,3,2,1,0:T(8,128)} %copy.42), calls=%async_computation.1 | async-start | bytes 1572864 | tf_op jit(solution)/shard_map/all_to_all | solution.py:120
  101.3 0.6 fusion.74
  101.9 2.1 %cosine_bitcast_fusion = (f32[16,16,512,1]{2,0,1,3:T(8,128)S(1)}, f32[16,16,512,1]{2,0,1,3:T(8,128)S(1)}) fusion(s32[16,16]{0,1:T(8,128)S(1)} %multiply_add_fusion.4), kind=kLoop, calls=%fused_computation.55 | loop fusion | flops 1966080 | bytes 1049600 | tf_op jit(solution)/shard_map/cos | solution.py:13
  104.0 21.1 %all-to-all-done.1 = f32[16,2,3,16,128]{4,3,2,1,0:T(8,128)S(1)} async-done(((f32[16,2,3,16,128]{4,3,2,1,0:T(8,128)}), f32[16,2,3,16,128]{4,3,2,1,0:T(8,128)S(1)}, u32[]{:S(2)}, u32[]{:S(2)}) %all-to-all-start.1) | async-done | bytes 786464 | tf_op jit(solution)/shard_map/all_to_all | solution.py:120
  125.1 1.1 convolution_bitcast_fusion
  126.2 1.1 fusion.9
  127.4 1.1 copy.47
  (26 shorter events, 3.2 us)
Async XLA Ops:
  0.6 6.1 %copy-start = (s32[6,512,128]{2,1,0:T(8,128)S(1)}, s32[6,512,128]{2,1,0:T(8,128)}, u32[]{:S(2)}) copy-start(s32[6,512,128]{2,1,0:T(8,128)} %param.1) | copy-start | bytes 4718596
  13.5 61.8 %all-to-all-start = ((f32[16,2,6,16,128]{4,3,2,1,0:T(8,128)}), f32[16,2,6,16,128]{4,3,2,1,0:T(8,128)S(1)}, u32[]{:S(2)}, u32[]{:S(2)}) async-start(f32[16,2,6,16,128]{4,3,2,1,0:T(8,128)} %copy.34), calls=%async_computation | async-start | bytes 3145728 | tf_op jit(solution)/shard_map/all_to_all | solution.py:58
  88.9 36.2 %all-to-all-start.1 = ((f32[16,2,3,16,128]{4,3,2,1,0:T(8,128)}), f32[16,2,3,16,128]{4,3,2,1,0:T(8,128)S(1)}, u32[]{:S(2)}, u32[]{:S(2)}) async-start(f32[16,2,3,16,128]{4,3,2,1,0:T(8,128)} %copy.42), calls=%async_computation.1 | async-start | bytes 1572864 | tf_op jit(solution)/shard_map/all_to_all | solution.py:120
where the time goes:
time: 129 us
  waiting for transfers between devices  66 us (51%)
  starting transfers between devices  28.2 us (22%)
  matrix products  23.9 us (19%)
  local copies, waits for them, and re-layouts  5.64 us (4%)
  other arithmetic  4.55 us (4%)
    all_to_all x1, waiting for transfers between devices, body(): received = lax.all_to_all(send, ('row', 'col'), 0, 0, tiled=True)  44.9 us
    all_to_all x1, waiting for transfers between devices, body(): pieces = lax.all_to_all(outgoing, ('row', 'col'), 0, 0, tiled=True)  21.1 us
    dot_general x12, matrix products, mixing(): return jnp.einsum(formula, former, latter, precision=highest)  20.7 us
    all_to_all x1, starting transfers between devices, body(): received = lax.all_to_all(send, ('row', 'col'), 0, 0, tiled=True)  16 us
    all_to_all x1, starting transfers between devices, body(): pieces = lax.all_to_all(outgoing, ('row', 'col'), 0, 0, tiled=True)  12.2 us
    cos x3, other arithmetic, phases(): return (jnp.cos(angles), -jnp.sin(angles))  3.33 us
  transfers between devices with their start and end apart: 2, of which 2 were waited for; matrix products, arithmetic and copies ran while one was open for 3% of the time, Pallas kernels for 0%

commit v1 on v0

--- a/solution.py
+++ b/solution.py
@@ -3,6 +3,8 @@
 import jax
 import jax.numpy as jnp
 from jax import lax
+from jax.experimental import pallas as pl
+from jax.experimental.pallas import tpu as pltpu
 from jax.sharding import PartitionSpec as P
 
 highest = lax.Precision.HIGHEST
@@ -26,6 +28,42 @@
     return ar * br - ai * bi, ar * bi + ai * br
 
 
+def row_kernel(limbs_ref, matrix_ref, turn_cos_ref, turn_sin_ref, out_ref):
+    half = turn_cos_ref.shape[0]
+    groups, _, _, local, narrow = out_ref.shape
+    values = (limbs_ref[0] - 32768).astype(jnp.float32) * (1.0 / 32768.0)
+    rows = jnp.dot(matrix_ref[...], values, precision=highest, preferred_element_type=jnp.float32)
+    real_rows = rows[:half]
+    imag_rows = rows[half:]
+    turn_cos = turn_cos_ref[...]
+    turn_sin = turn_sin_ref[...]
+    out_ref[:, 0, 0] = (real_rows * turn_cos - imag_rows * turn_sin).reshape(groups, local, narrow)
+    out_ref[:, 1, 0] = (real_rows * turn_sin + imag_rows * turn_cos).reshape(groups, local, narrow)
+
+
+def row_stage(limbs, matrix, turn_cos, turn_sin, groups):
+    number, height, narrow = limbs.shape
+    half = turn_cos.shape[0]
+    local = half // groups
+    return pl.pallas_call(
+        row_kernel,
+        out_shape=jax.ShapeDtypeStruct((groups, 2, number, local, narrow), jnp.float32),
+        grid=(number,),
+        in_specs=[
+            pl.BlockSpec((1, height, narrow), lambda i: (i, 0, 0)),
+            pl.BlockSpec((2 * half, height), lambda i: (0, 0)),
+            pl.BlockSpec((half, narrow), lambda i: (0, 0)),
+            pl.BlockSpec((half, narrow), lambda i: (0, 0)),
+        ],
+        out_specs=pl.BlockSpec((groups, 2, 1, local, narrow), lambda i: (0, 0, i, 0, 0)),
+        cost_estimate=pl.CostEstimate(
+            flops=6 * 2 * 2 * half * height * narrow * number,
+            transcendentals=0,
+            bytes_accessed=4 * (3 * number * height * narrow + 2 * half * height),
+        ),
+    )(limbs, matrix, turn_cos, turn_sin)
+
+
 def body(limbs):
     groups = lax.axis_size(("row", "col"))
     number, height, narrow = limbs.shape
@@ -34,27 +72,21 @@
     half = height // 2
     local = half // groups
     device = lax.axis_index(("row", "col"))
-    balanced = (limbs - 32768).astype(jnp.float32) / 32768.0
 
     half_index = jnp.arange(half, dtype=jnp.int32)
     row_index = jnp.arange(height, dtype=jnp.int32)
     row_cos, row_sin = phases(
         row_index[None, :] * (2 * half_index[:, None] + 1) % (2 * height), height
     )
-    columns = device * narrow + jnp.arange(narrow, dtype=jnp.int32)
-    turn_cos, turn_sin = phases(
-        columns[None, :] * (2 * half_index[:, None] + 1) % (2 * limb_total), limb_total
-    )
+    base_cos, base_sin = phases(device * narrow * (2 * half_index + 1), limb_total)
+    lane_index = jnp.arange(narrow, dtype=jnp.int32)
+    lane_cos, lane_sin = phases(lane_index[None, :] * (2 * half_index[:, None] + 1), limb_total)
+    base_cos = base_cos[:, None]
+    base_sin = base_sin[:, None]
+    turn_cos = base_cos * lane_cos - base_sin * lane_sin
+    turn_sin = base_cos * lane_sin + base_sin * lane_cos
 
-    real_rows = mixing(row_cos, balanced, "ja,iab->ijb")
-    imag_rows = mixing(row_sin, balanced, "ja,iab->ijb")
-    turned = jnp.stack(
-        (
-            real_rows * turn_cos - imag_rows * turn_sin,
-            real_rows * turn_sin + imag_rows * turn_cos,
-        )
-    )
-    send = turned.reshape(2, number, groups, local, narrow).transpose(2, 0, 1, 3, 4)
+    send = row_stage(limbs, jnp.concatenate((row_cos, row_sin), axis=0), turn_cos, turn_sin, groups)
     received = lax.all_to_all(send, ("row", "col"), 0, 0, tiled=True)
 
     outer_cos, outer_sin = dft_table(groups)

time: 129 us -> 128 us (level)
  the two profiles are of different devices: /device:TPU:8 before, /device:TPU:10 now
where the time goes in v1:
time: 128 us
  waiting for transfers between devices  65.7 us (51%)
  starting transfers between devices  28.2 us (22%)
  matrix products  13.1 us (10%)
  Pallas kernels  8.51 us (7%)
  other arithmetic  8.47 us (7%)
  local copies, waits for them, and re-layouts  3.87 us (3%)
    all_to_all x1, waiting for transfers between devices, body(): received = lax.all_to_all(send, ('row', 'col'), 0, 0, tiled=True)  44.9 us
    all_to_all x1, waiting for transfers between devices, body(): pieces = lax.all_to_all(outgoing, ('row', 'col'), 0, 0, tiled=True)  20.9 us
    all_to_all x1, starting transfers between devices, body(): received = lax.all_to_all(send, ('row', 'col'), 0, 0, tiled=True)  16 us
    all_to_all x1, starting transfers between devices, body(): pieces = lax.all_to_all(outgoing, ('row', 'col'), 0, 0, tiled=True)  12.2 us
    dot_general x10, matrix products, mixing(): return jnp.einsum(formula, former, latter, precision=highest)  9.87 us
    pallas_call x1, Pallas kernels, row_stage(): pl.pallas_call(row_kernel, out_shape=jax.ShapeDtypeStruct((groups, 2, num...  8.51 us
    cos x2, other arithmetic, phases(): return (jnp.cos(angles), -jnp.sin(angles))  4.3 us
  transfers between devices with their start and end apart: 2, of which 2 were waited for; matrix products, arithmetic and copies ran while one was open for 3% of the time, Pallas kernels for 0%

profile of v1, /device:TPU:10, one launch (start us, length us, event | category | flops | bytes accessed | tf_op | source)
XLA Modules:
  0.0 128.1 jit_solution(755100099067580652)
XLA Ops:
  0.1 2.1 %fusion.37 = (f32[256,512]{1,0:T(8,128)S(1)}, f32[256,512]{1,0:T(8,128)S(1)}) fusion(s32[256]{0:T(256)S(1)} %multiply_add_fusion.6), kind=kLoop, calls=%fused_computation.64 | loop fusion | flops 1966080 | bytes 1049600 | tf_op jit(solution)/shard_map/cos | solution.py:15
  2.2 1.3 %multiply_add_fusion.4 = (f32[256,128]{1,0:T(8,128)}, f32[256,128]{1,0:T(8,128)}) fusion(f32[256]{0:T(256)S(1)} %get-tuple-element.31, s32[256]{0:T(256)S(1)} %multiply_add_fusion.6, f32[256]{0:T(256)S(1)} %get-tuple-element.32), kind=kLoop, calls=%fused_computation.80 | loop fusion | flops 327680 | bytes 265216 | tf_op jit(solution)/shard_map/add | solution.py:87
  3.5 1.1 pad_maximum_fusion.matrix_ref
  4.6 8.5 %shard_map.17 = f32[16,2,6,16,128]{4,3,2,1,0:T(8,128)} custom-call(s32[6,512,128]{2,1,0:T(8,128)} %limbs_ref.1, f32[512,512]{1,0:T(8,128)} %pad_maximum_fusion.matrix_ref, f32[256,128]{1,0:T(8,128)} %get-tuple-element.26.turn_cos_ref, f32[256,128]{1,0:T(8,128)} %get-tuple-element.25.turn_sin_ref), custom_call_target="tpu_custom_call" | custom-call | flops 2415919104 | bytes 5767168 | tf_op jit(solution)/shard_map/pallas_call | solution.py:48
  13.1 16.0 %all-to-all-start = ((f32[16,2,6,16,128]{4,3,2,1,0:T(8,128)}), f32[16,2,6,16,128]{4,3,2,1,0:T(8,128)S(1)}, u32[]{:S(2)}, u32[]{:S(2)}) async-start(f32[16,2,6,16,128]{4,3,2,1,0:T(8,128)} %shard_map.17), calls=%async_computation | async-start | bytes 3145728 | tf_op jit(solution)/shard_map/all_to_all | solution.py:90
  30.0 44.9 %all-to-all-done = f32[16,2,6,16,128]{4,3,2,1,0:T(8,128)S(1)} async-done(((f32[16,2,6,16,128]{4,3,2,1,0:T(8,128)}), f32[16,2,6,16,128]{4,3,2,1,0:T(8,128)S(1)}, u32[]{:S(2)}, u32[]{:S(2)}) %all-to-all-start) | async-done | bytes 1572896 | tf_op jit(solution)/shard_map/all_to_all | solution.py:90
  75.5 2.3 %fusion = f32[16,2,6,16,128]{4,0,3,2,1:T(8,128)S(1)} fusion(f32[6,16,128,32]{2,1,0,3:T(8,128)S(1)} %bitcast.110, f32[16,1,32]{2,0,1:T(8,128)S(1)} %copy.22, f32[16,1,32]{2,0,1:T(8,128)S(1)} %copy.21), kind=kOutput, calls=%fused_computation | convolution fusion | flops 150995968 | bytes 3149824 | tf_op jit(solution)/shard_map/dot_general | solution.py:100
  78.0 1.2 fusion.13
  79.1 1.2 fusion.11
  80.3 1.2 convolution_subtract_fusion
  81.5 1.2 convolution_add_fusion
  82.9 0.7 fusion.36
  83.6 0.7 fusion.35
  84.3 0.7 convolution_subtract_fusion.1
  85.1 0.8 add_bitcast_fusion
  86.5 0.9 fusion.6
  87.4 1.1 copy.30
  88.5 12.2 %all-to-all-start.1 = ((f32[16,2,3,16,128]{4,3,2,1,0:T(8,128)}), f32[16,2,3,16,128]{4,3,2,1,0:T(8,128)S(1)}, u32[]{:S(2)}, u32[]{:S(2)}) async-start(f32[16,2,3,16,128]{4,3,2,1,0:T(8,128)} %copy.30), calls=%async_computation.1 | async-start | bytes 1572864 | tf_op jit(solution)/shard_map/all_to_all | solution.py:152
  101.0 0.6 multiply_subtract_fusion.1
  101.6 2.1 %cosine_bitcast_fusion = (f32[16,16,512,1]{2,0,1,3:T(8,128)S(1)}, f32[16,16,512,1]{2,0,1,3:T(8,128)S(1)}) fusion(s32[16,16]{0,1:T(8,128)S(1)} %multiply_add_fusion.5), kind=kLoop, calls=%fused_computation.42 | loop fusion | flops 1966080 | bytes 1049600 | tf_op jit(solution)/shard_map/cos | solution.py:15
  103.8 20.9 %all-to-all-done.1 = f32[16,2,3,16,128]{4,3,2,1,0:T(8,128)S(1)} async-done(((f32[16,2,3,16,128]{4,3,2,1,0:T(8,128)}), f32[16,2,3,16,128]{4,3,2,1,0:T(8,128)S(1)}, u32[]{:S(2)}, u32[]{:S(2)}) %all-to-all-start.1) | async-done | bytes 786464 | tf_op jit(solution)/shard_map/all_to_all | solution.py:152
  124.7 1.1 convolution_bitcast_fusion
  125.8 1.1 fusion.5
  127.0 1.1 copy.37
  (24 shorter events, 2.8 us)
Async XLA Ops:
  13.1 61.8 %all-to-all-start = ((f32[16,2,6,16,128]{4,3,2,1,0:T(8,128)}), f32[16,2,6,16,128]{4,3,2,1,0:T(8,128)S(1)}, u32[]{:S(2)}, u32[]{:S(2)}) async-start(f32[16,2,6,16,128]{4,3,2,1,0:T(8,128)} %shard_map.17), calls=%async_computation | async-start | bytes 3145728 | tf_op jit(solution)/shard_map/all_to_all | solution.py:90
  88.5 36.1 %all-to-all-start.1 = ((f32[16,2,3,16,128]{4,3,2,1,0:T(8,128)}), f32[16,2,3,16,128]{4,3,2,1,0:T(8,128)S(1)}, u32[]{:S(2)}, u32[]{:S(2)}) async-start(f32[16,2,3,16,128]{4,3,2,1,0:T(8,128)} %copy.30), calls=%async_computation.1 | async-start | bytes 1572864 | tf_op jit(solution)/shard_map/all_to_all | solution.py:152

commit v2 on v1

--- a/solution.py
+++ b/solution.py
@@ -2,6 +2,8 @@
 
 import jax
 import jax.numpy as jnp
+import ml_dtypes
+import numpy as np
 from jax import lax
 from jax.experimental import pallas as pl
 from jax.experimental.pallas import tpu as pltpu
@@ -15,9 +17,25 @@
     return (jnp.cos(angles), -jnp.sin(angles))
 
 
+def exact_phases(multiple, period):
+    angles = np.asarray(multiple, dtype=np.float64) * (math.pi / period)
+    return np.cos(angles), -np.sin(angles)
+
+
+def constant(table):
+    return jnp.asarray(np.asarray(table, dtype=np.float32))
+
+
 def dft_table(length):
-    indices = jnp.arange(length, dtype=jnp.int32)
-    return phases(2 * (indices[:, None] * indices[None, :] % length), length)
+    indices = np.arange(length, dtype=np.int64)
+    table_cos, table_sin = exact_phases(2 * (indices[:, None] * indices[None, :] % length), length)
+    return constant(table_cos), constant(table_sin)
+
+
+def split_bf16(table):
+    first = table.astype(ml_dtypes.bfloat16)
+    second = (table - first.astype(np.float64)).astype(ml_dtypes.bfloat16)
+    return np.concatenate((first, second), axis=0)
 
 
 def mixing(former, latter, formula):
@@ -31,8 +49,16 @@
 def row_kernel(limbs_ref, matrix_ref, turn_cos_ref, turn_sin_ref, out_ref):
     half = turn_cos_ref.shape[0]
     groups, _, _, local, narrow = out_ref.shape
-    values = (limbs_ref[0] - 32768).astype(jnp.float32) * (1.0 / 32768.0)
-    rows = jnp.dot(matrix_ref[...], values, precision=highest, preferred_element_type=jnp.float32)
+    centred = limbs_ref[0] - jnp.int32(32768)
+    upper = lax.shift_right_arithmetic(centred, jnp.int32(8))
+    lower = centred - upper * jnp.int32(256)
+    pieces = jnp.concatenate((upper, lower), axis=1).astype(jnp.float32).astype(jnp.bfloat16)
+    products = jnp.dot(matrix_ref[...], pieces, preferred_element_type=jnp.float32)
+    count = 2 * half
+    narrow_in = pieces.shape[1] // 2
+    upper_part = products[:count, :narrow_in] + products[count:, :narrow_in]
+    lower_part = products[:count, narrow_in:] + products[count:, narrow_in:]
+    rows = (upper_part * 256.0 + lower_part) * (1.0 / 32768.0)
     real_rows = rows[:half]
     imag_rows = rows[half:]
     turn_cos = turn_cos_ref[...]
@@ -51,15 +77,15 @@
         grid=(number,),
         in_specs=[
             pl.BlockSpec((1, height, narrow), lambda i: (i, 0, 0)),
-            pl.BlockSpec((2 * half, height), lambda i: (0, 0)),
+            pl.BlockSpec((4 * half, height), lambda i: (0, 0)),
             pl.BlockSpec((half, narrow), lambda i: (0, 0)),
             pl.BlockSpec((half, narrow), lambda i: (0, 0)),
         ],
         out_specs=pl.BlockSpec((groups, 2, 1, local, narrow), lambda i: (0, 0, i, 0, 0)),
         cost_estimate=pl.CostEstimate(
-            flops=6 * 2 * 2 * half * height * narrow * number,
+            flops=2 * 4 * half * height * 2 * narrow * number,
             transcendentals=0,
-            bytes_accessed=4 * (3 * number * height * narrow + 2 * half * height),
+            bytes_accessed=4 * 3 * number * height * narrow + 2 * 4 * half * height,
         ),
     )(limbs, matrix, turn_cos, turn_sin)
 
@@ -73,20 +99,29 @@
     local = half // groups
     device = lax.axis_index(("row", "col"))
 
-    half_index = jnp.arange(half, dtype=jnp.int32)
-    row_index = jnp.arange(height, dtype=jnp.int32)
-    row_cos, row_sin = phases(
+    half_index = np.arange(half, dtype=np.int64)
+    row_index = np.arange(height, dtype=np.int64)
+    row_cos_exact, row_sin_exact = exact_phases(
         row_index[None, :] * (2 * half_index[:, None] + 1) % (2 * height), height
     )
-    base_cos, base_sin = phases(device * narrow * (2 * half_index + 1), limb_total)
-    lane_index = jnp.arange(narrow, dtype=jnp.int32)
-    lane_cos, lane_sin = phases(lane_index[None, :] * (2 * half_index[:, None] + 1), limb_total)
+    row_matrix = jnp.asarray(split_bf16(np.concatenate((row_cos_exact, row_sin_exact), axis=0)))
+    row_pieces = lax.optimization_barrier(row_matrix)
+    row_float = row_pieces[: 2 * half].astype(jnp.float32) + row_pieces[2 * half :].astype(jnp.float32)
+    row_cos = row_float[:half]
+    row_sin = row_float[half:]
+    base_cos, base_sin = phases(
+        device * narrow * (2 * jnp.arange(half, dtype=jnp.int32) + 1), limb_total
+    )
+    lane_index = np.arange(narrow, dtype=np.int64)
+    lane_cos, lane_sin = exact_phases(lane_index[None, :] * (2 * half_index[:, None] + 1), limb_total)
+    lane_cos = constant(lane_cos)
+    lane_sin = constant(lane_sin)
     base_cos = base_cos[:, None]
     base_sin = base_sin[:, None]
     turn_cos = base_cos * lane_cos - base_sin * lane_sin
     turn_sin = base_cos * lane_sin + base_sin * lane_cos
 
-    send = row_stage(limbs, jnp.concatenate((row_cos, row_sin), axis=0), turn_cos, turn_sin, groups)
+    send = row_stage(limbs, row_matrix, turn_cos, turn_sin, groups)
     received = lax.all_to_all(send, ("row", "col"), 0, 0, tiled=True)
 
     outer_cos, outer_sin = dft_table(groups)
@@ -100,13 +135,13 @@
     mixed = jnp.dot(
         forward_block, received.reshape(2 * groups, -1), precision=highest
     ).reshape(groups, 2, number, local, narrow)
-    outer_index = jnp.arange(groups, dtype=jnp.int32)
-    inner_index = jnp.arange(narrow, dtype=jnp.int32)
-    twist_cos, twist_sin = phases(
+    outer_index = np.arange(groups, dtype=np.int64)
+    inner_index = np.arange(narrow, dtype=np.int64)
+    twist_cos, twist_sin = exact_phases(
         2 * (outer_index[:, None] * inner_index[None, :] % breadth), breadth
     )
-    twist_cos = twist_cos[:, None, None, :]
-    twist_sin = twist_sin[:, None, None, :]
+    twist_cos = constant(twist_cos)[:, None, None, :]
+    twist_sin = constant(twist_sin)[:, None, None, :]
     mixed_re = mixed[:, 0]
     mixed_im = mixed[:, 1]
     turned_re = mixed_re * twist_cos - mixed_im * twist_sin

time: 128 us -> 111 us (0.87)
  blocking collectives: 0 us -> 57.2 us
  waiting for transfers between devices: 65.7 us -> 23.6 us
  starting transfers between devices: 28.2 us -> 5.63 us
  other arithmetic: 8.47 us -> 2.46 us
  matrix products: 13.1 us -> 10.6 us
  Pallas kernels: 8.51 us -> 6.24 us
    all_to_all x0 -> x1, blocking collectives: none -> 57.2 us  [body(): received = lax.all_to_all(send, ('row', 'col'), 0, 0, tiled=True)]
    all_to_all x1 -> x0, waiting for transfers between devices: 44.9 us -> none  [body(): received = lax.all_to_all(send, ('row', 'col'), 0, 0, tiled=True)]
    all_to_all x1 -> x0, starting transfers between devices: 16 us -> none  [body(): received = lax.all_to_all(send, ('row', 'col'), 0, 0, tiled=True)]
    all_to_all x1, starting transfers between devices: 12.2 us -> 5.63 us  [body(): pieces = lax.all_to_all(outgoing, ('row', 'col'), 0, 0, tiled=True)]
    cos x2 -> x0, other arithmetic: 4.3 us -> none  [phases(): return (jnp.cos(angles), -jnp.sin(angles))]
    all_to_all x1, waiting for transfers between devices: 20.9 us -> 23.6 us  [body(): pieces = lax.all_to_all(outgoing, ('row', 'col'), 0, 0, tiled=True)]
    dot_general x10, matrix products: 9.87 us -> 7.42 us  [mixing(): return jnp.einsum(formula, former, latter, precision=highest)]
    pallas_call x1, Pallas kernels: 8.51 us -> 6.24 us  [row_stage(): pl.pallas_call(row_kernel, out_shape=jax.ShapeDtypeStruct((groups, 2, num...]
  transfers between devices with their start and end apart: 2 -> 1, of which waited for: 2 -> 1; matrix products, arithmetic and copies ran while one was open for 3% -> 0% of each run, Pallas kernels for 0% -> 0%
where the time goes in v2:
time: 111 us
  blocking collectives  57.2 us (52%)
  waiting for transfers between devices  23.6 us (21%)
  matrix products  10.6 us (10%)
  Pallas kernels  6.24 us (6%)
  starting transfers between devices  5.63 us (5%)
  local copies, waits for them, and re-layouts  4.76 us (4%)
  other arithmetic  2.46 us (2%)
    all_to_all x1, blocking collectives, body(): received = lax.all_to_all(send, ('row', 'col'), 0, 0, tiled=True)  57.2 us
    all_to_all x1, waiting for transfers between devices, body(): pieces = lax.all_to_all(outgoing, ('row', 'col'), 0, 0, tiled=True)  23.6 us
    dot_general x10, matrix products, mixing(): return jnp.einsum(formula, former, latter, precision=highest)  7.42 us
    pallas_call x1, Pallas kernels, row_stage(): pl.pallas_call(row_kernel, out_shape=jax.ShapeDtypeStruct((groups, 2, num...  6.24 us
    all_to_all x1, starting transfers between devices, body(): pieces = lax.all_to_all(outgoing, ('row', 'col'), 0, 0, tiled=True)  5.63 us
    dot_general x1, matrix products, body(): jnp.dot(forward_block, received.reshape(2 * groups, -1), precision=highest)  2.28 us
  transfers between devices with their start and end apart: 1, of which 1 were waited for; matrix products, arithmetic and copies ran while one was open for 0% of the time, Pallas kernels for 0%

profile of v2, /device:TPU:10, one launch (start us, length us, event | category | flops | bytes accessed | tf_op | source)
XLA Modules:
  0.0 110.9 jit_solution(17725383232821041163)
XLA Ops:
  0.0 1.8 %multiply_add_fusion.3 = (f32[256,128]{1,0:T(8,128)}, f32[256,128]{1,0:T(8,128)}) fusion(f32[256,128]{1,0:T(8,128)} %constant.40.clone, f32[256,128]{1,0:T(8,128)} %constant.41.clone, f32[256]{0:T(256)S(1)} %get-tuple-element.19, f32[256]{0:T(256)S(1)} %get-tuple-element.20), kind=kLoop, calls=%fused_computation.51 | loop fusion | flops 196608 | bytes 526336 | tf_op jit(solution)/shard_map/add | solution.py:122
  1.9 6.2 %shard_map.100 = f32[16,2,6,16,128]{4,3,2,1,0:T(8,128)} custom-call(s32[6,512,128]{2,1,0:T(8,128)} %limbs_ref.1, bf16[1024,512]{1,0:T(8,128)(2,1)} %constant.39.clone.matrix_ref, f32[256,128]{1,0:T(8,128)} %get-tuple-element.18.turn_cos_ref, f32[256,128]{1,0:T(8,128)} %get-tuple-element.17.turn_sin_ref), custom_call_target="tpu_custom_call" | custom-call | flops 1610612736 | bytes 5767168 | tf_op jit(solution)/shard_map/pallas_call | solution.py:74
  8.1 57.2 %all_to_all.10 = f32[16,2,6,16,128]{4,3,2,1,0:T(8,128)S(1)} all-to-all(f32[16,2,6,16,128]{4,3,2,1,0:T(8,128)} %shard_map.100), channel_id=1, replica_groups=mesh['pair'=32,'row'=2,'col'=8] {'row','col'}, dimensions={0} | all-to-all | bytes 3145728 | tf_op jit(solution)/shard_map/all_to_all | solution.py:125
  65.3 0.3 reshape.49
  65.6 0.3 copy.59
  65.9 0.4 copy-done.8
  66.3 2.3 %fusion = f32[16,2,6,16,128]{4,0,3,2,1:T(8,128)S(1)} fusion(f32[16,2,32,1,1]{2,0,4,3,1:T(8,128)S(1)} %copy-done.8, f32[6,16,128,32]{2,1,0,3:T(8,128)S(1)} %bitcast.104), kind=kOutput, calls=%fused_computation | convolution fusion | flops 150994944 | bytes 3149824 | tf_op jit(solution)/shard_map/dot_general | solution.py:135
  68.9 0.6 copy-done.4
  69.5 0.9 fusion.13
  70.4 0.9 fusion.11
  71.4 0.9 convolution_subtract_fusion
  72.3 0.9 convolution_add_fusion
  73.5 0.5 fusion.22
  74.0 0.5 fusion.21
  74.5 0.5 convolution_subtract_fusion.1
  75.0 0.5 add_bitcast_fusion
  75.9 0.4 copy-done.7
  76.4 0.9 fusion.6
  77.3 1.1 %copy.39 = f32[16,2,3,16,128]{4,3,2,1,0:T(8,128)} copy(f32[16,2,3,16,128]{4,0,3,2,1:T(8,128)S(1)} %fusion.6) | data formatting | bytes 1572864 | tf_op jit(solution)/shard_map/dot_general | solution.py:182
  78.5 5.6 %all-to-all-start.1 = ((f32[16,2,3,16,128]{4,3,2,1,0:T(8,128)}), f32[16,2,3,16,128]{4,3,2,1,0:T(8,128)S(1)}, u32[]{:S(2)}, u32[]{:S(2)}) async-start(f32[16,2,3,16,128]{4,3,2,1,0:T(8,128)} %copy.39), calls=%async_computation.1 | async-start | bytes 1572864 | tf_op jit(solution)/shard_map/all_to_all | solution.py:187
  84.3 23.6 %all-to-all-done.1 = f32[16,2,3,16,128]{4,3,2,1,0:T(8,128)S(1)} async-done(((f32[16,2,3,16,128]{4,3,2,1,0:T(8,128)}), f32[16,2,3,16,128]{4,3,2,1,0:T(8,128)S(1)}, u32[]{:S(2)}, u32[]{:S(2)}) %all-to-all-start.1) | async-done | bytes 786464 | tf_op jit(solution)/shard_map/all_to_all | solution.py:187
  108.0 0.9 convolution_bitcast_fusion
  108.8 0.9 fusion.5
  109.7 1.1 %copy.45 = f32[3,512,128]{2,1,0:T(8,128)} copy(f32[3,512,128]{1,2,0:T(8,128)S(1)} %fusion.5) | data formatting | bytes 1572864 | tf_op jit(solution)/shard_map/mul | solution.py:199
  (25 shorter events, 1.1 us)
Async XLA Ops:
  65.6 0.7 copy-start.8
  66.3 2.3 %copy-start.5 = (f32[16,128]{1,0:T(8,128)S(1)}, f32[16,128]{1,0:T(8,128)}, u32[]{:S(2)}) copy-start(f32[16,128]{1,0:T(8,128)} %constant.44.clone) | copy-start | bytes 24580
  66.3 2.3 %copy-start.6 = (f32[16,128]{1,0:T(8,128)S(1)}, f32[16,128]{1,0:T(8,128)}, u32[]{:S(2)}) copy-start(f32[16,128]{1,0:T(8,128)} %constant.45.clone) | copy-start | bytes 24580
  68.7 0.8 copy-start.4
  68.9 1.6 %copy-start.2 = (f32[128,128,1,1]{1,0,3,2:T(8,128)S(1)}, f32[128,128,1,1]{1,0,3,2:T(8,128)}, u32[]{:S(2)}) copy-start(f32[128,128,1,1]{1,0,3,2:T(8,128)} %constant.65) | copy-start | bytes 196612
  75.6 0.7 copy-start.7
  77.3 6.8 %copy-start.3 = (bf16[1024,512]{1,0:T(8,128)(2,1)S(1)}, bf16[1024,512]{1,0:T(8,128)(2,1)}, u32[]{:S(2)}) copy-start(bf16[1024,512]{1,0:T(8,128)(2,1)} %constant.39.clone.matrix_ref) | copy-start | bytes 3145732
  78.5 29.5 %all-to-all-start.1 = ((f32[16,2,3,16,128]{4,3,2,1,0:T(8,128)}), f32[16,2,3,16,128]{4,3,2,1,0:T(8,128)S(1)}, u32[]{:S(2)}, u32[]{:S(2)}) async-start(f32[16,2,3,16,128]{4,3,2,1,0:T(8,128)} %copy.39), calls=%async_computation.1 | async-start | bytes 1572864 | tf_op jit(solution)/shard_map/all_to_all | solution.py:187
  84.2 23.7 %copy-start = (f32[256,128]{1,0:T(8,128)S(1)}, f32[256,128]{1,0:T(8,128)}, u32[]{:S(2)}) copy-start(f32[256,128]{1,0:T(8,128)} %get-tuple-element.17.turn_sin_ref) | copy-start | bytes 393220
  84.2 23.7 %copy-start.1 = (f32[256,128]{1,0:T(8,128)S(1)}, f32[256,128]{1,0:T(8,128)}, u32[]{:S(2)}) copy-start(f32[256,128]{1,0:T(8,128)} %get-tuple-element.18.turn_cos_ref) | copy-start | bytes 393220

commit v3 on v2

--- a/solution.py
+++ b/solution.py
@@ -90,6 +90,117 @@
     )(limbs, matrix, turn_cos, turn_sin)
 
 
+def fft16(real, imag, sign):
+    def dft4(a, b, c, d):
+        sum_ac = (a[0] + c[0], a[1] + c[1])
+        dif_ac = (a[0] - c[0], a[1] - c[1])
+        sum_bd = (b[0] + d[0], b[1] + d[1])
+        dif_bd = (b[0] - d[0], b[1] - d[1])
+        return (
+            (sum_ac[0] + sum_bd[0], sum_ac[1] + sum_bd[1]),
+            (dif_ac[0] - sign * dif_bd[1], dif_ac[1] + sign * dif_bd[0]),
+            (sum_ac[0] - sum_bd[0], sum_ac[1] - sum_bd[1]),
+            (dif_ac[0] + sign * dif_bd[1], dif_ac[1] - sign * dif_bd[0]),
+        )
+
+    values = list(zip(real, imag))
+    stage = []
+    for first in range(4):
+        outs = dft4(*(values[4 * second + first] for second in range(4)))
+        turned = []
+        for low, (re, im) in enumerate(outs):
+            if first * low == 0:
+                turned.append((re, im))
+                continue
+            angle = sign * 2.0 * math.pi * first * low / 16.0
+            cos_v, sin_v = math.cos(angle), math.sin(angle)
+            turned.append((re * cos_v - im * sin_v, re * sin_v + im * cos_v))
+        stage.append(turned)
+    result = [None] * 16
+    for low in range(4):
+        outs = dft4(*(stage[first][low] for first in range(4)))
+        for high in range(4):
+            result[low + 4 * high] = outs[high]
+    return [v[0] for v in result], [v[1] for v in result]
+
+
+def column_kernel(in_ref, twist_cos_ref, twist_sin_ref, forward_ref, inverse_ref, out_ref, lifted_ref, mixed_ref):
+    groups, _, number, local, narrow = in_ref.shape
+    tile = 8
+    for operand in range(number):
+        for start in range(0, local, tile):
+            rows = pl.ds(start, tile)
+            real = [in_ref[p, 0, operand, rows, :] for p in range(groups)]
+            imag = [in_ref[p, 1, operand, rows, :] for p in range(groups)]
+            real, imag = fft16(real, imag, -1.0)
+            for k in range(groups):
+                cos_v = twist_cos_ref[k : k + 1, :]
+                sin_v = twist_sin_ref[k : k + 1, :]
+                lifted_ref[k, operand, rows, :narrow] = real[k] * cos_v - imag[k] * sin_v
+                lifted_ref[k, operand, rows, narrow:] = real[k] * sin_v + imag[k] * cos_v
+    spectra = jnp.dot(
+        lifted_ref[...].reshape(groups * number * local, 2 * narrow),
+        forward_ref[...],
+        precision=highest,
+        preferred_element_type=jnp.float32,
+    ).reshape(groups, number, local, 2 * narrow)
+
+    def spectrum(k):
+        part = spectra[:, k]
+        return part[..., :narrow], part[..., narrow:]
+
+    first = multiply_pair(*spectrum(0), *spectrum(3))
+    second = multiply_pair(*spectrum(1), *spectrum(4))
+    third_a = multiply_pair(*spectrum(2), *spectrum(4))
+    third_b = multiply_pair(*spectrum(0), *spectrum(5))
+    combined = (first, second, (third_a[0] + third_b[0], third_a[1] + third_b[1]))
+    for index, (re, im) in enumerate(combined):
+        mixed_ref[:, index, :, :narrow] = re
+        mixed_ref[:, index, :, narrow:] = im
+    outputs = mixed_ref.shape[1]
+    mixed_ref[...] = jnp.dot(
+        mixed_ref[...].reshape(groups * outputs * local, 2 * narrow),
+        inverse_ref[...],
+        precision=highest,
+        preferred_element_type=jnp.float32,
+    ).reshape(groups, outputs, local, 2 * narrow)
+    for operand in range(outputs):
+        for start in range(0, local, tile):
+            rows = pl.ds(start, tile)
+            real = []
+            imag = []
+            for k in range(groups):
+                re = mixed_ref[k, operand, rows, :narrow]
+                im = mixed_ref[k, operand, rows, narrow:]
+                cos_v = twist_cos_ref[k : k + 1, :]
+                sin_v = twist_sin_ref[k : k + 1, :]
+                real.append(re * cos_v + im * sin_v)
+                imag.append(im * cos_v - re * sin_v)
+            real, imag = fft16(real, imag, 1.0)
+            for p in range(groups):
+                out_ref[p, 0, operand, rows, :] = real[p]
+                out_ref[p, 1, operand, rows, :] = imag[p]
+
+
+def column_stage(received, twist_cos, twist_sin, forward, inverse):
+    groups, _, number, local, narrow = received.shape
+    outputs = 3
+    rows = groups * local
+    return pl.pallas_call(
+        column_kernel,
+        out_shape=jax.ShapeDtypeStruct((groups, 2, outputs, local, narrow), jnp.float32),
+        scratch_shapes=[
+            pltpu.VMEM((groups, number, local, 2 * narrow), jnp.float32),
+            pltpu.VMEM((groups, outputs, local, 2 * narrow), jnp.float32),
+        ],
+        cost_estimate=pl.CostEstimate(
+            flops=6 * 2 * rows * (number + outputs) * (2 * narrow) ** 2,
+            transcendentals=0,
+            bytes_accessed=4 * rows * narrow * 2 * (number + outputs),
+        ),
+    )(received, twist_cos, twist_sin, forward, inverse)
+
+
 def body(limbs):
     groups = lax.axis_size(("row", "col"))
     number, height, narrow = limbs.shape
@@ -124,66 +235,17 @@
     send = row_stage(limbs, row_matrix, turn_cos, turn_sin, groups)
     received = lax.all_to_all(send, ("row", "col"), 0, 0, tiled=True)
 
-    outer_cos, outer_sin = dft_table(groups)
-    forward_block = jnp.stack(
-        (
-            jnp.stack((outer_cos, -outer_sin), -1),
-            jnp.stack((outer_sin, outer_cos), -1),
-        ),
-        1,
-    ).reshape(2 * groups, 2 * groups)
-    mixed = jnp.dot(
-        forward_block, received.reshape(2 * groups, -1), precision=highest
-    ).reshape(groups, 2, number, local, narrow)
     outer_index = np.arange(groups, dtype=np.int64)
     inner_index = np.arange(narrow, dtype=np.int64)
     twist_cos, twist_sin = exact_phases(
         2 * (outer_index[:, None] * inner_index[None, :] % breadth), breadth
     )
-    twist_cos = constant(twist_cos)[:, None, None, :]
-    twist_sin = constant(twist_sin)[:, None, None, :]
-    mixed_re = mixed[:, 0]
-    mixed_im = mixed[:, 1]
-    turned_re = mixed_re * twist_cos - mixed_im * twist_sin
-    turned_im = mixed_re * twist_sin + mixed_im * twist_cos
-    inner_cos, inner_sin = dft_table(narrow)
-    spec_re = mixing(turned_re, inner_cos, "kijq,qm->kijm") - mixing(
-        turned_im, inner_sin, "kijq,qm->kijm"
-    )
-    spec_im = mixing(turned_re, inner_sin, "kijq,qm->kijm") + mixing(
-        turned_im, inner_cos, "kijq,qm->kijm"
-    )
-
-    def spectrum(k):
-        return spec_re[:, k], spec_im[:, k]
-
-    first = multiply_pair(*spectrum(0), *spectrum(3))
-    second = multiply_pair(*spectrum(1), *spectrum(4))
-    third_a = multiply_pair(*spectrum(2), *spectrum(4))
-    third_b = multiply_pair(*spectrum(0), *spectrum(5))
-    comb_re = jnp.stack((first[0], second[0], third_a[0] + third_b[0]), axis=1)
-    comb_im = jnp.stack((first[1], second[1], third_a[1] + third_b[1]), axis=1)
-
-    back_re = mixing(comb_re, inner_cos, "kijm,qm->kijq") + mixing(
-        comb_im, inner_sin, "kijm,qm->kijq"
-    )
-    back_im = mixing(comb_im, inner_cos, "kijm,qm->kijq") - mixing(
-        comb_re, inner_sin, "kijm,qm->kijq"
-    )
-    untwist_re = back_re * twist_cos + back_im * twist_sin
-    untwist_im = back_im * twist_cos - back_re * twist_sin
-    inverse_block = jnp.stack(
-        (
-            jnp.stack((outer_cos, outer_sin), -1),
-            jnp.stack((-outer_sin, outer_cos), -1),
-        ),
-        1,
-    ).reshape(2 * groups, 2 * groups)
-    outgoing = jnp.dot(
-        inverse_block,
-        jnp.stack((untwist_re, untwist_im), axis=1).reshape(2 * groups, -1),
-        precision=highest,
-    ).reshape(groups, 2, 3, local, narrow)
+    inner_cos, inner_sin = exact_phases(2 * (inner_index[:, None] * inner_index[None, :] % narrow), narrow)
+    forward = np.block([[inner_cos, inner_sin], [-inner_sin, inner_cos]])
+    inverse = np.block([[inner_cos, -inner_sin], [inner_sin, inner_cos]])
+    outgoing = column_stage(
+        received, constant(twist_cos), constant(twist_sin), constant(forward), constant(inverse)
+    )
     pieces = lax.all_to_all(outgoing, ("row", "col"), 0, 0, tiled=True)
 
     turn_cos = turn_cos.reshape(groups, 1, local, narrow)

time: 111 us -> 105 us (0.946)
  the two profiles are of different devices: /device:TPU:10 before, /device:TPU:14 now
where the time goes in v3:
time: 105 us; the launch traced here: 104 us
  blocking collectives  57.3 us (55%)
  waiting for transfers between devices  23.6 us (22%)
  Pallas kernels  12.4 us (12%)
  starting transfers between devices  5.76 us (5%)
  other arithmetic  2 us (2%)
  matrix products  1.72 us (2%)
  local copies, waits for them, and re-layouts  1.23 us (1%)
    all_to_all x1, blocking collectives, body(): received = lax.all_to_all(send, ('row', 'col'), 0, 0, tiled=True)  57.3 us
    all_to_all x1, waiting for transfers between devices, body(): pieces = lax.all_to_all(outgoing, ('row', 'col'), 0, 0, tiled=True)  23.6 us
    pallas_call x1, Pallas kernels, row_stage(): pl.pallas_call(row_kernel, out_shape=jax.ShapeDtypeStruct((groups, 2, num...  6.29 us
    pallas_call x1, Pallas kernels, column_stage(): pl.pallas_call(column_kernel, out_shape=jax.ShapeDtypeStruct((groups, 2,...  6.07 us
    all_to_all x1, starting transfers between devices, body(): pieces = lax.all_to_all(outgoing, ('row', 'col'), 0, 0, tiled=True)  5.76 us
  transfers between devices with their start and end apart: 1, of which 1 were waited for; matrix products, arithmetic and copies ran while one was open for 0% of the time, Pallas kernels for 0%

profile of v3, /device:TPU:14, one launch (start us, length us, event | category | flops | bytes accessed | tf_op | source)
XLA Modules:
  0.0 104.1 jit_solution(17677960740140977307)
XLA Ops:
  0.0 1.8 %multiply_add_fusion = (f32[256,128]{1,0:T(8,128)}, f32[256,128]{1,0:T(8,128)}) fusion(f32[256,128]{1,0:T(8,128)} %constant.36.clone, f32[256,128]{1,0:T(8,128)} %constant.37.clone, f32[256]{0:T(256)S(1)} %get-tuple-element.9, f32[256]{0:T(256)S(1)} %get-tuple-element.10), kind=kLoop, calls=%fused_computation.18 | loop fusion | flops 196608 | bytes 526336 | tf_op jit(solution)/shard_map/add | solution.py:233
  1.9 6.3 %shard_map.82 = f32[16,2,6,16,128]{4,3,2,1,0:T(8,128)} custom-call(s32[6,512,128]{2,1,0:T(8,128)} %limbs_ref.1, bf16[1024,512]{1,0:T(8,128)(2,1)} %constant.35.clone.matrix_ref, f32[256,128]{1,0:T(8,128)} %get-tuple-element.8.turn_cos_ref, f32[256,128]{1,0:T(8,128)} %get-tuple-element.7.turn_sin_ref), custom_call_target="tpu_custom_call" | custom-call | flops 1610612736 | bytes 5767168 | tf_op jit(solution)/shard_map/pallas_call | solution.py:74
  8.2 57.3 %all_to_all.10.in_ref = f32[16,2,6,16,128]{4,3,2,1,0:T(8,128)} all-to-all(f32[16,2,6,16,128]{4,3,2,1,0:T(8,128)} %shard_map.82), channel_id=1, replica_groups=mesh['pair'=32,'row'=2,'col'=8] {'row','col'}, dimensions={0} | all-to-all | bytes 3145728 | tf_op jit(solution)/shard_map/all_to_all | solution.py:236
  65.5 6.1 %shard_map.83 = f32[16,2,3,16,128]{4,3,2,1,0:T(8,128)} custom-call(f32[16,2,6,16,128]{4,3,2,1,0:T(8,128)} %all_to_all.10.in_ref, f32[16,128]{1,0:T(8,128)} %constant.38.clone.twist_cos_ref, f32[16,128]{1,0:T(8,128)} %constant.39.clone.twist_sin_ref, f32[256,256]{1,0:T(8,128)} %constant.40.clone.forward_ref, f32[256,256]{1,0:T(8,128)} %constant.41.clone.inverse_ref), custom_call_target="tpu_custom_call" | custom-call | flops 1811939328 | bytes 2359296 | tf_op jit(solution)/shard_map/pallas_call | solution.py:189
  71.6 0.0 copy-start.2
  71.6 5.8 %all-to-all-start.1 = ((f32[16,2,3,16,128]{4,3,2,1,0:T(8,128)}), f32[16,2,3,16,128]{4,3,2,1,0:T(8,128)S(1)}, u32[]{:S(2)}, u32[]{:S(2)}) async-start(f32[16,2,3,16,128]{4,3,2,1,0:T(8,128)} %shard_map.83), calls=%async_computation.1 | async-start | bytes 1572864 | tf_op jit(solution)/shard_map/all_to_all | solution.py:249
  77.3 0.0 copy-done.2
  77.3 0.1 convert_add_fusion
  77.5 0.0 copy-start
  77.5 0.0 copy-start.1
  77.5 0.1 fusion.14
  77.6 23.6 %all-to-all-done.1 = f32[16,2,3,16,128]{4,3,2,1,0:T(8,128)S(1)} async-done(((f32[16,2,3,16,128]{4,3,2,1,0:T(8,128)}), f32[16,2,3,16,128]{4,3,2,1,0:T(8,128)S(1)}, u32[]{:S(2)}, u32[]{:S(2)}) %all-to-all-start.1) | async-done | bytes 786464 | tf_op jit(solution)/shard_map/all_to_all | solution.py:249
  101.2 0.0 copy-done
  101.2 0.0 copy-done.1
  101.2 0.9 convolution_bitcast_fusion
  102.1 0.9 fusion.2
  103.0 1.1 %copy.14 = f32[3,512,128]{2,1,0:T(8,128)} copy(f32[3,512,128]{1,2,0:T(8,128)S(1)} %fusion.2) | data formatting | bytes 1572864 | tf_op jit(solution)/shard_map/mul | solution.py:261
  (1 shorter events, 0.0 us)
Async XLA Ops:
  71.6 5.8 %copy-start.2 = (bf16[1024,512]{1,0:T(8,128)(2,1)S(1)}, bf16[1024,512]{1,0:T(8,128)(2,1)}, u32[]{:S(2)}) copy-start(bf16[1024,512]{1,0:T(8,128)(2,1)} %constant.35.clone.matrix_ref) | copy-start | bytes 3145732
  71.6 29.6 %all-to-all-start.1 = ((f32[16,2,3,16,128]{4,3,2,1,0:T(8,128)}), f32[16,2,3,16,128]{4,3,2,1,0:T(8,128)S(1)}, u32[]{:S(2)}, u32[]{:S(2)}) async-start(f32[16,2,3,16,128]{4,3,2,1,0:T(8,128)} %shard_map.83), calls=%async_computation.1 | async-start | bytes 1572864 | tf_op jit(solution)/shard_map/all_to_all | solution.py:249
  77.5 23.7 %copy-start = (f32[256,128]{1,0:T(8,128)S(1)}, f32[256,128]{1,0:T(8,128)}, u32[]{:S(2)}) copy-start(f32[256,128]{1,0:T(8,128)} %get-tuple-element.7.turn_sin_ref) | copy-start | bytes 393220
  77.5 23.7 %copy-start.1 = (f32[256,128]{1,0:T(8,128)S(1)}, f32[256,128]{1,0:T(8,128)}, u32[]{:S(2)}) copy-start(f32[256,128]{1,0:T(8,128)} %get-tuple-element.8.turn_cos_ref) | copy-start | bytes 393220

commit v4 on v3

--- a/solution.py
+++ b/solution.py
@@ -1,3 +1,4 @@
+import functools
 import math
 
 import jax
@@ -46,48 +47,91 @@
     return ar * br - ai * bi, ar * bi + ai * br
 
 
-def row_kernel(limbs_ref, matrix_ref, turn_cos_ref, turn_sin_ref, out_ref):
-    half = turn_cos_ref.shape[0]
+def row_kernel(limbs_ref, matrix_ref, base_cos_ref, base_sin_ref, lane_cos_ref, lane_sin_ref, out_ref):
+    number = limbs_ref.shape[0]
+    half = lane_cos_ref.shape[0]
     groups, _, _, local, narrow = out_ref.shape
-    centred = limbs_ref[0] - jnp.int32(32768)
-    upper = lax.shift_right_arithmetic(centred, jnp.int32(8))
-    lower = centred - upper * jnp.int32(256)
-    pieces = jnp.concatenate((upper, lower), axis=1).astype(jnp.float32).astype(jnp.bfloat16)
+    turn_cos, turn_sin = turn_tables(base_cos_ref, base_sin_ref, lane_cos_ref, lane_sin_ref)
+    centred = [limbs_ref[i] - jnp.int32(32768) for i in range(number)]
+    upper = [lax.shift_right_arithmetic(value, jnp.int32(8)) for value in centred]
+    lower = [value - top * jnp.int32(256) for value, top in zip(centred, upper)]
+    pieces = jnp.concatenate(upper + lower, axis=1).astype(jnp.float32).astype(jnp.bfloat16)
     products = jnp.dot(matrix_ref[...], pieces, preferred_element_type=jnp.float32)
     count = 2 * half
-    narrow_in = pieces.shape[1] // 2
-    upper_part = products[:count, :narrow_in] + products[count:, :narrow_in]
-    lower_part = products[:count, narrow_in:] + products[count:, narrow_in:]
+    width = number * narrow
+    upper_part = products[:count, :width] + products[count:, :width]
+    lower_part = products[:count, width:] + products[count:, width:]
     rows = (upper_part * 256.0 + lower_part) * (1.0 / 32768.0)
-    real_rows = rows[:half]
-    imag_rows = rows[half:]
-    turn_cos = turn_cos_ref[...]
-    turn_sin = turn_sin_ref[...]
-    out_ref[:, 0, 0] = (real_rows * turn_cos - imag_rows * turn_sin).reshape(groups, local, narrow)
-    out_ref[:, 1, 0] = (real_rows * turn_sin + imag_rows * turn_cos).reshape(groups, local, narrow)
-
-
-def row_stage(limbs, matrix, turn_cos, turn_sin, groups):
+    for i in range(number):
+        real_rows = rows[:half, i * narrow : (i + 1) * narrow]
+        imag_rows = rows[half:, i * narrow : (i + 1) * narrow]
+        out_ref[:, 0, i] = (real_rows * turn_cos - imag_rows * turn_sin).reshape(groups, local, narrow)
+        out_ref[:, 1, i] = (real_rows * turn_sin + imag_rows * turn_cos).reshape(groups, local, narrow)
+
+
+def turn_tables(base_cos_ref, base_sin_ref, lane_cos_ref, lane_sin_ref):
+    base_cos = base_cos_ref[...]
+    base_sin = base_sin_ref[...]
+    lane_cos = lane_cos_ref[...]
+    lane_sin = lane_sin_ref[...]
+    return base_cos * lane_cos - base_sin * lane_sin, base_cos * lane_sin + base_sin * lane_cos
+
+
+def row_stage(limbs, matrix, tables, groups):
     number, height, narrow = limbs.shape
-    half = turn_cos.shape[0]
+    half = tables[2].shape[0]
     local = half // groups
     return pl.pallas_call(
         row_kernel,
         out_shape=jax.ShapeDtypeStruct((groups, 2, number, local, narrow), jnp.float32),
-        grid=(number,),
-        in_specs=[
-            pl.BlockSpec((1, height, narrow), lambda i: (i, 0, 0)),
-            pl.BlockSpec((4 * half, height), lambda i: (0, 0)),
-            pl.BlockSpec((half, narrow), lambda i: (0, 0)),
-            pl.BlockSpec((half, narrow), lambda i: (0, 0)),
-        ],
-        out_specs=pl.BlockSpec((groups, 2, 1, local, narrow), lambda i: (0, 0, i, 0, 0)),
         cost_estimate=pl.CostEstimate(
             flops=2 * 4 * half * height * 2 * narrow * number,
             transcendentals=0,
             bytes_accessed=4 * 3 * number * height * narrow + 2 * 4 * half * height,
         ),
-    )(limbs, matrix, turn_cos, turn_sin)
+    )(limbs, matrix, *tables)
+
+
+def final_kernel(pieces_ref, matrix_ref, base_cos_ref, base_sin_ref, lane_cos_ref, lane_sin_ref, out_ref, *, scale):
+    groups, _, outputs, local, narrow = pieces_ref.shape
+    half = groups * local
+    turn_cos, turn_sin = turn_tables(base_cos_ref, base_sin_ref, lane_cos_ref, lane_sin_ref)
+    turn_cos = turn_cos.reshape(groups, local, narrow)
+    turn_sin = turn_sin.reshape(groups, local, narrow)
+    columns = []
+    for i in range(outputs):
+        real = pieces_ref[:, 0, i]
+        imag = pieces_ref[:, 1, i]
+        untwisted = jnp.stack(
+            (real * turn_cos + imag * turn_sin, imag * turn_cos - real * turn_sin), axis=1
+        )
+        columns.append(untwisted.reshape(2 * half, narrow))
+    gathered = jnp.concatenate(columns, axis=1)
+    first = gathered.astype(jnp.bfloat16)
+    second = (gathered - first.astype(jnp.float32)).astype(jnp.bfloat16)
+    products = jnp.dot(
+        matrix_ref[...], jnp.concatenate((first, second), axis=1), preferred_element_type=jnp.float32
+    )
+    height = matrix_ref.shape[0] // 2
+    width = outputs * narrow
+    small = products[height:, width:] + products[height:, :width] + products[:height, width:]
+    total = (small + products[:height, :width]) * scale
+    for i in range(outputs):
+        out_ref[i] = total[:, i * narrow : (i + 1) * narrow]
+
+
+def final_stage(pieces, matrix, tables, scale):
+    groups, _, outputs, local, narrow = pieces.shape
+    height = matrix.shape[0] // 2
+    return pl.pallas_call(
+        functools.partial(final_kernel, scale=scale),
+        out_shape=jax.ShapeDtypeStruct((outputs, height, narrow), jnp.float32),
+        cost_estimate=pl.CostEstimate(
+            flops=2 * 4 * height * height * 2 * outputs * narrow,
+            transcendentals=0,
+            bytes_accessed=4 * 3 * outputs * height * narrow + 2 * 2 * height * height,
+        ),
+    )(pieces, matrix, *tables)
 
 
 def fft16(real, imag, sign):
@@ -216,23 +260,18 @@
         row_index[None, :] * (2 * half_index[:, None] + 1) % (2 * height), height
     )
     row_matrix = jnp.asarray(split_bf16(np.concatenate((row_cos_exact, row_sin_exact), axis=0)))
-    row_pieces = lax.optimization_barrier(row_matrix)
-    row_float = row_pieces[: 2 * half].astype(jnp.float32) + row_pieces[2 * half :].astype(jnp.float32)
-    row_cos = row_float[:half]
-    row_sin = row_float[half:]
+    final_table = np.stack(
+        (row_cos_exact.reshape(groups, local, height), row_sin_exact.reshape(groups, local, height)), axis=1
+    ).reshape(2 * half, height)
+    final_matrix = jnp.asarray(split_bf16(final_table.T))
     base_cos, base_sin = phases(
         device * narrow * (2 * jnp.arange(half, dtype=jnp.int32) + 1), limb_total
     )
     lane_index = np.arange(narrow, dtype=np.int64)
     lane_cos, lane_sin = exact_phases(lane_index[None, :] * (2 * half_index[:, None] + 1), limb_total)
-    lane_cos = constant(lane_cos)
-    lane_sin = constant(lane_sin)
-    base_cos = base_cos[:, None]
-    base_sin = base_sin[:, None]
-    turn_cos = base_cos * lane_cos - base_sin * lane_sin
-    turn_sin = base_cos * lane_sin + base_sin * lane_cos
-
-    send = row_stage(limbs, row_matrix, turn_cos, turn_sin, groups)
+    tables = (base_cos[:, None], base_sin[:, None], constant(lane_cos), constant(lane_sin))
+
+    send = row_stage(limbs, row_matrix, tables, groups)
     received = lax.all_to_all(send, ("row", "col"), 0, 0, tiled=True)
 
     outer_index = np.arange(groups, dtype=np.int64)
@@ -248,17 +287,8 @@
     )
     pieces = lax.all_to_all(outgoing, ("row", "col"), 0, 0, tiled=True)
 
-    turn_cos = turn_cos.reshape(groups, 1, local, narrow)
-    turn_sin = turn_sin.reshape(groups, 1, local, narrow)
-    real_part = pieces[:, 0] * turn_cos + pieces[:, 1] * turn_sin
-    imag_part = pieces[:, 1] * turn_cos - pieces[:, 0] * turn_sin
     scale_factor = 2.0 / (limb_total * math.sqrt(limb_total))
-    row_cos = row_cos.reshape(groups, local, height)
-    row_sin = row_sin.reshape(groups, local, height)
-    total = mixing(row_cos, real_part, "sja,sijb->iab") + mixing(
-        row_sin, imag_part, "sja,sijb->iab"
-    )
-    return total * scale_factor
+    return final_stage(pieces, final_matrix, tables, scale_factor)
 
 
 def solution(mesh):

time: 105 us -> 104 us (level)
  the two profiles are of different devices: /device:TPU:14 before, /device:TPU:12 now
where the time goes in v4:
time: 104 us
  blocking collectives  87.7 us (84%)
  Pallas kernels  14.6 us (14%)
  other arithmetic  1.22 us (1%)
    all_to_all x1, blocking collectives, body(): received = lax.all_to_all(send, ('row', 'col'), 0, 0, tiled=True)  57.3 us
    all_to_all x1, blocking collectives, body(): pieces = lax.all_to_all(outgoing, ('row', 'col'), 0, 0, tiled=True)  30.4 us
    pallas_call x1, Pallas kernels, column_stage(): pl.pallas_call(column_kernel, out_shape=jax.ShapeDtypeStruct((groups, 2,...  6.07 us
    pallas_call x1, Pallas kernels, row_stage(): pl.pallas_call(row_kernel, out_shape=jax.ShapeDtypeStruct((groups, 2, num...  4.95 us
    pallas_call x1, Pallas kernels, final_stage(): pl.pallas_call(functools.partial(final_kernel, scale=scale), out_shape=ja...  3.6 us

profile of v4, /device:TPU:12, one launch (start us, length us, event | category | flops | bytes accessed | tf_op | source)
XLA Modules:
  0.0 103.5 jit_solution(15244114959038268411)
XLA Ops:
  0.0 1.2 %sine_negate_fusion = (f32[256,1]{1,0:T(8,128)}, f32[256,1]{1,0:T(8,128)}) fusion(s32[]{:T(128)S(6)} %mul.58), kind=kLoop, calls=%fused_computation | loop fusion | flops 1536 | bytes 2052 | tf_op jit(solution)/shard_map/neg | solution.py:18
  1.2 4.9 %shard_map.91 = f32[16,2,6,16,128]{4,3,2,1,0:T(8,128)} custom-call(s32[6,512,128]{2,1,0:T(8,128)} %limbs_ref.1, bf16[1024,512]{1,0:T(8,128)(2,1)} %constant.35.clone.matrix_ref, f32[256,1]{1,0:T(8,128)} %get-tuple-element.6.base_cos_ref, f32[256,1]{1,0:T(8,128)} %get-tuple-element.5.base_sin_ref, f32[256,128]{1,0:T(8,128)} %constant.37.clone.lane_cos_ref, ...), custom_call_target="tpu_custom_call" | custom-call | flops 1610612736 | bytes 5767168 | tf_op jit(solution)/shard_map/pallas_call | solution.py:84
  6.2 57.3 %all_to_all.10.in_ref = f32[16,2,6,16,128]{4,3,2,1,0:T(8,128)} all-to-all(f32[16,2,6,16,128]{4,3,2,1,0:T(8,128)} %shard_map.91), channel_id=1, replica_groups=mesh['pair'=32,'row'=2,'col'=8] {'row','col'}, dimensions={0} | all-to-all | bytes 3145728 | tf_op jit(solution)/shard_map/all_to_all | solution.py:275
  63.5 6.1 %shard_map.92 = f32[16,2,3,16,128]{4,3,2,1,0:T(8,128)} custom-call(f32[16,2,6,16,128]{4,3,2,1,0:T(8,128)} %all_to_all.10.in_ref, f32[16,128]{1,0:T(8,128)} %constant.39.clone.twist_cos_ref, f32[16,128]{1,0:T(8,128)} %constant.40.clone.twist_sin_ref, f32[256,256]{1,0:T(8,128)} %constant.41.clone.forward_ref, f32[256,256]{1,0:T(8,128)} %constant.42.clone.inverse_ref), custom_call_target="tpu_custom_call" | custom-call | flops 1811939328 | bytes 2359296 | tf_op jit(solution)/shard_map/pallas_call | solution.py:233
  69.6 30.4 %all_to_all.11.pieces_ref = f32[16,2,3,16,128]{4,3,2,1,0:T(8,128)} all-to-all(f32[16,2,3,16,128]{4,3,2,1,0:T(8,128)} %shard_map.92), channel_id=1, replica_groups=mesh['pair'=32,'row'=2,'col'=8] {'row','col'}, dimensions={0} | all-to-all | bytes 1572864 | tf_op jit(solution)/shard_map/all_to_all | solution.py:288
  99.9 3.6 %shard_map.93 = f32[3,512,128]{2,1,0:T(8,128)} custom-call(f32[16,2,3,16,128]{4,3,2,1,0:T(8,128)} %all_to_all.11.pieces_ref, bf16[1024,512]{1,0:T(8,128)(2,1)} %constant.36.clone.matrix_ref, f32[256,1]{1,0:T(8,128)} %get-tuple-element.6.base_cos_ref, f32[256,1]{1,0:T(8,128)} %get-tuple-element.5.base_sin_ref, f32[256,128]{1,0:T(8,128)} %constant.37.clone.lane_cos_ref, ...), custom_call_target="tpu_custom_call" | custom-call | flops 1610612736 | bytes 3407872 | tf_op jit(solution)/shard_map/pallas_call | solution.py:126

commit v5 on v4

--- a/solution.py
+++ b/solution.py
@@ -168,6 +168,18 @@
     return [v[0] for v in result], [v[1] for v in result]
 
 
+def split_dot(values, matrix_ref):
+    size = matrix_ref.shape[0] // 2
+    first = values.astype(jnp.bfloat16)
+    second = (values - first.astype(jnp.float32)).astype(jnp.bfloat16)
+    major = matrix_ref[:size]
+    minor = matrix_ref[size:]
+    small = jnp.dot(second, major, preferred_element_type=jnp.float32) + jnp.dot(
+        first, minor, preferred_element_type=jnp.float32
+    )
+    return small + jnp.dot(first, major, preferred_element_type=jnp.float32)
+
+
 def column_kernel(in_ref, twist_cos_ref, twist_sin_ref, forward_ref, inverse_ref, out_ref, lifted_ref, mixed_ref):
     groups, _, number, local, narrow = in_ref.shape
     tile = 8
@@ -182,11 +194,8 @@
                 sin_v = twist_sin_ref[k : k + 1, :]
                 lifted_ref[k, operand, rows, :narrow] = real[k] * cos_v - imag[k] * sin_v
                 lifted_ref[k, operand, rows, narrow:] = real[k] * sin_v + imag[k] * cos_v
-    spectra = jnp.dot(
-        lifted_ref[...].reshape(groups * number * local, 2 * narrow),
-        forward_ref[...],
-        precision=highest,
-        preferred_element_type=jnp.float32,
+    spectra = split_dot(
+        lifted_ref[...].reshape(groups * number * local, 2 * narrow), forward_ref
     ).reshape(groups, number, local, 2 * narrow)
 
     def spectrum(k):
@@ -202,11 +211,8 @@
         mixed_ref[:, index, :, :narrow] = re
         mixed_ref[:, index, :, narrow:] = im
     outputs = mixed_ref.shape[1]
-    mixed_ref[...] = jnp.dot(
-        mixed_ref[...].reshape(groups * outputs * local, 2 * narrow),
-        inverse_ref[...],
-        precision=highest,
-        preferred_element_type=jnp.float32,
+    mixed_ref[...] = split_dot(
+        mixed_ref[...].reshape(groups * outputs * local, 2 * narrow), inverse_ref
     ).reshape(groups, outputs, local, 2 * narrow)
     for operand in range(outputs):
         for start in range(0, local, tile):
@@ -238,7 +244,7 @@
             pltpu.VMEM((groups, outputs, local, 2 * narrow), jnp.float32),
         ],
         cost_estimate=pl.CostEstimate(
-            flops=6 * 2 * rows * (number + outputs) * (2 * narrow) ** 2,
+            flops=3 * 2 * rows * (number + outputs) * (2 * narrow) ** 2,
             transcendentals=0,
             bytes_accessed=4 * rows * narrow * 2 * (number + outputs),
         ),
@@ -264,9 +270,12 @@
         (row_cos_exact.reshape(groups, local, height), row_sin_exact.reshape(groups, local, height)), axis=1
     ).reshape(2 * half, height)
     final_matrix = jnp.asarray(split_bf16(final_table.T))
-    base_cos, base_sin = phases(
-        device * narrow * (2 * jnp.arange(half, dtype=jnp.int32) + 1), limb_total
-    )
+    device_index = np.arange(groups, dtype=np.int64)
+    base_cos, base_sin = exact_phases(
+        device_index[:, None] * narrow * (2 * half_index[None, :] + 1), limb_total
+    )
+    base_cos = lax.dynamic_index_in_dim(constant(base_cos), device, 0, keepdims=False)
+    base_sin = lax.dynamic_index_in_dim(constant(base_sin), device, 0, keepdims=False)
     lane_index = np.arange(narrow, dtype=np.int64)
     lane_cos, lane_sin = exact_phases(lane_index[None, :] * (2 * half_index[:, None] + 1), limb_total)
     tables = (base_cos[:, None], base_sin[:, None], constant(lane_cos), constant(lane_sin))
@@ -283,7 +292,11 @@
     forward = np.block([[inner_cos, inner_sin], [-inner_sin, inner_cos]])
     inverse = np.block([[inner_cos, -inner_sin], [inner_sin, inner_cos]])
     outgoing = column_stage(
-        received, constant(twist_cos), constant(twist_sin), constant(forward), constant(inverse)
+        received,
+        constant(twist_cos),
+        constant(twist_sin),
+        jnp.asarray(split_bf16(forward)),
+        jnp.asarray(split_bf16(inverse)),
     )
     pieces = lax.all_to_all(outgoing, ("row", "col"), 0, 0, tiled=True)
 

time: 104 us -> 103 us (level)
  the two profiles are of different devices: /device:TPU:12 before, /device:TPU:14 now
where the time goes in v5:
time: 103 us
  blocking collectives  87.7 us (85%)
  Pallas kernels  13 us (13%)
  local copies, waits for them, and re-layouts  2.31 us (2%)
    all_to_all x1, blocking collectives, body(): received = lax.all_to_all(send, ('row', 'col'), 0, 0, tiled=True)  57.3 us
    all_to_all x1, blocking collectives, body(): pieces = lax.all_to_all(outgoing, ('row', 'col'), 0, 0, tiled=True)  30.4 us
    pallas_call x1, Pallas kernels, row_stage(): pl.pallas_call(row_kernel, out_shape=jax.ShapeDtypeStruct((groups, 2, num...  4.95 us
    pallas_call x1, Pallas kernels, column_stage(): pl.pallas_call(column_kernel, out_shape=jax.ShapeDtypeStruct((groups, 2,...  4.41 us
    pallas_call x1, Pallas kernels, final_stage(): pl.pallas_call(functools.partial(final_kernel, scale=scale), out_shape=ja...  3.6 us

profile of v5, /device:TPU:14, one launch (start us, length us, event | category | flops | bytes accessed | tf_op | source)
XLA Modules:
  0.0 103.0 jit_solution(15014069412136821459)
XLA Ops:
  0.0 0.7 dynamic-slice_bitcast_fusion
  0.7 0.8 copy.13.base_sin_ref
  1.5 0.8 copy.12.base_cos_ref
  2.3 5.0 %shard_map.109 = f32[16,2,6,16,128]{4,3,2,1,0:T(8,128)} custom-call(s32[6,512,128]{2,1,0:T(8,128)} %limbs_ref.1, bf16[1024,512]{1,0:T(8,128)(2,1)} %constant.39.clone.matrix_ref, f32[256,1]{1,0:T(8,128)} %copy.12.base_cos_ref, f32[256,1]{1,0:T(8,128)} %copy.13.base_sin_ref, f32[256,128]{1,0:T(8,128)} %constant.43.clone.lane_cos_ref, ...), custom_call_target="tpu_custom_call" | custom-call | flops 1610612736 | bytes 5767168 | tf_op jit(solution)/shard_map/pallas_call | solution.py:84
  7.3 57.3 %all_to_all.10.in_ref = f32[16,2,6,16,128]{4,3,2,1,0:T(8,128)} all-to-all(f32[16,2,6,16,128]{4,3,2,1,0:T(8,128)} %shard_map.109), channel_id=1, replica_groups=mesh['pair'=32,'row'=2,'col'=8] {'row','col'}, dimensions={0} | all-to-all | bytes 3145728 | tf_op jit(solution)/shard_map/all_to_all | solution.py:284
  64.6 4.4 %shard_map.110 = f32[16,2,3,16,128]{4,3,2,1,0:T(8,128)} custom-call(f32[16,2,6,16,128]{4,3,2,1,0:T(8,128)} %all_to_all.10.in_ref, f32[16,128]{1,0:T(8,128)} %constant.45.clone.twist_cos_ref, f32[16,128]{1,0:T(8,128)} %constant.46.clone.twist_sin_ref, bf16[512,256]{1,0:T(8,128)(2,1)} %constant.47.clone.forward_ref, bf16[512,256]{1,0:T(8,128)(2,1)} %constant.48.clone.inverse_ref), custom_call_target="tpu_custom_call" | custom-call | flops 905969664 | bytes 2359296 | tf_op jit(solution)/shard_map/pallas_call | solution.py:239
  69.0 30.4 %all_to_all.11.pieces_ref = f32[16,2,3,16,128]{4,3,2,1,0:T(8,128)} all-to-all(f32[16,2,3,16,128]{4,3,2,1,0:T(8,128)} %shard_map.110), channel_id=1, replica_groups=mesh['pair'=32,'row'=2,'col'=8] {'row','col'}, dimensions={0} | all-to-all | bytes 1572864 | tf_op jit(solution)/shard_map/all_to_all | solution.py:301
  99.4 3.6 %shard_map.111 = f32[3,512,128]{2,1,0:T(8,128)} custom-call(f32[16,2,3,16,128]{4,3,2,1,0:T(8,128)} %all_to_all.11.pieces_ref, bf16[1024,512]{1,0:T(8,128)(2,1)} %constant.40.clone.matrix_ref, f32[256,1]{1,0:T(8,128)} %copy.12.base_cos_ref, f32[256,1]{1,0:T(8,128)} %copy.13.base_sin_ref, f32[256,128]{1,0:T(8,128)} %constant.43.clone.lane_cos_ref, ...), custom_call_target="tpu_custom_call" | custom-call | flops 1610612736 | bytes 3407872 | tf_op jit(solution)/shard_map/pallas_call | solution.py:126

commit v6 on v5

--- a/solution.py
+++ b/solution.py
@@ -47,11 +47,11 @@
     return ar * br - ai * bi, ar * bi + ai * br
 
 
-def row_kernel(limbs_ref, matrix_ref, base_cos_ref, base_sin_ref, lane_cos_ref, lane_sin_ref, out_ref):
+def row_kernel(limbs_ref, matrix_ref, turn_cos_ref, turn_sin_ref, out_ref):
     number = limbs_ref.shape[0]
-    half = lane_cos_ref.shape[0]
+    half = turn_cos_ref.shape[0]
     groups, _, _, local, narrow = out_ref.shape
-    turn_cos, turn_sin = turn_tables(base_cos_ref, base_sin_ref, lane_cos_ref, lane_sin_ref)
+    turn_cos, turn_sin = turn_tables(turn_cos_ref, turn_sin_ref)
     centred = [limbs_ref[i] - jnp.int32(32768) for i in range(number)]
     upper = [lax.shift_right_arithmetic(value, jnp.int32(8)) for value in centred]
     lower = [value - top * jnp.int32(256) for value, top in zip(centred, upper)]
@@ -69,17 +69,13 @@
         out_ref[:, 1, i] = (real_rows * turn_sin + imag_rows * turn_cos).reshape(groups, local, narrow)
 
 
-def turn_tables(base_cos_ref, base_sin_ref, lane_cos_ref, lane_sin_ref):
-    base_cos = base_cos_ref[...]
-    base_sin = base_sin_ref[...]
-    lane_cos = lane_cos_ref[...]
-    lane_sin = lane_sin_ref[...]
-    return base_cos * lane_cos - base_sin * lane_sin, base_cos * lane_sin + base_sin * lane_cos
+def turn_tables(turn_cos_ref, turn_sin_ref):
+    return turn_cos_ref[...], turn_sin_ref[...]
 
 
 def row_stage(limbs, matrix, tables, groups):
     number, height, narrow = limbs.shape
-    half = tables[2].shape[0]
+    half = tables[0].shape[0]
     local = half // groups
     return pl.pallas_call(
         row_kernel,
@@ -92,20 +88,24 @@
     )(limbs, matrix, *tables)
 
 
-def final_kernel(pieces_ref, matrix_ref, base_cos_ref, base_sin_ref, lane_cos_ref, lane_sin_ref, out_ref, *, scale):
+def final_kernel(pieces_ref, matrix_ref, turn_cos_ref, turn_sin_ref, out_ref, *, scale):
     groups, _, outputs, local, narrow = pieces_ref.shape
     half = groups * local
-    turn_cos, turn_sin = turn_tables(base_cos_ref, base_sin_ref, lane_cos_ref, lane_sin_ref)
+    turn_cos, turn_sin = turn_tables(turn_cos_ref, turn_sin_ref)
     turn_cos = turn_cos.reshape(groups, local, narrow)
     turn_sin = turn_sin.reshape(groups, local, narrow)
     columns = []
     for i in range(outputs):
         real = pieces_ref[:, 0, i]
         imag = pieces_ref[:, 1, i]
-        untwisted = jnp.stack(
-            (real * turn_cos + imag * turn_sin, imag * turn_cos - real * turn_sin), axis=1
+        untwisted = jnp.concatenate(
+            (
+                (real * turn_cos + imag * turn_sin).reshape(half, narrow),
+                (imag * turn_cos - real * turn_sin).reshape(half, narrow),
+            ),
+            axis=0,
         )
-        columns.append(untwisted.reshape(2 * half, narrow))
+        columns.append(untwisted)
     gathered = jnp.concatenate(columns, axis=1)
     first = gathered.astype(jnp.bfloat16)
     second = (gathered - first.astype(jnp.float32)).astype(jnp.bfloat16)
@@ -266,19 +266,21 @@
         row_index[None, :] * (2 * half_index[:, None] + 1) % (2 * height), height
     )
     row_matrix = jnp.asarray(split_bf16(np.concatenate((row_cos_exact, row_sin_exact), axis=0)))
-    final_table = np.stack(
-        (row_cos_exact.reshape(groups, local, height), row_sin_exact.reshape(groups, local, height)), axis=1
-    ).reshape(2 * half, height)
-    final_matrix = jnp.asarray(split_bf16(final_table.T))
+    final_matrix = jnp.asarray(split_bf16(np.concatenate((row_cos_exact, row_sin_exact), axis=0).T))
     device_index = np.arange(groups, dtype=np.int64)
     base_cos, base_sin = exact_phases(
         device_index[:, None] * narrow * (2 * half_index[None, :] + 1), limb_total
     )
-    base_cos = lax.dynamic_index_in_dim(constant(base_cos), device, 0, keepdims=False)
-    base_sin = lax.dynamic_index_in_dim(constant(base_sin), device, 0, keepdims=False)
+    base_cos = lax.dynamic_index_in_dim(constant(base_cos), device, 0, keepdims=False)[:, None]
+    base_sin = lax.dynamic_index_in_dim(constant(base_sin), device, 0, keepdims=False)[:, None]
     lane_index = np.arange(narrow, dtype=np.int64)
     lane_cos, lane_sin = exact_phases(lane_index[None, :] * (2 * half_index[:, None] + 1), limb_total)
-    tables = (base_cos[:, None], base_sin[:, None], constant(lane_cos), constant(lane_sin))
+    lane_cos = constant(lane_cos)
+    lane_sin = constant(lane_sin)
+    tables = (
+        base_cos * lane_cos - base_sin * lane_sin,
+        base_cos * lane_sin + base_sin * lane_cos,
+    )
 
     send = row_stage(limbs, row_matrix, tables, groups)
     received = lax.all_to_all(send, ("row", "col"), 0, 0, tiled=True)

time: 103 us -> 103 us (level)
  other arithmetic: 0 us -> 1.8 us
  local copies, waits for them, and re-layouts: 2.31 us -> 0.72 us
    broadcast_in_dim x3 -> x0, local copies, waits for them, and re-layouts: 2.31 us -> none  [the longest x2 1.51 us: body(): base_sin[:, None]]
    add x0 -> x1, other arithmetic: none -> 1.8 us  [body(): base_cos * lane_sin + base_sin * lane_cos]
where the time goes in v6:
time: 103 us
  blocking collectives  87.7 us (85%)
  Pallas kernels  12.7 us (12%)
  other arithmetic  1.8 us (2%)
    all_to_all x1, blocking collectives, body(): received = lax.all_to_all(send, ('row', 'col'), 0, 0, tiled=True)  57.3 us
    all_to_all x1, blocking collectives, body(): pieces = lax.all_to_all(outgoing, ('row', 'col'), 0, 0, tiled=True)  30.4 us
    pallas_call x1, Pallas kernels, row_stage(): pl.pallas_call(row_kernel, out_shape=jax.ShapeDtypeStruct((groups, 2, num...  4.85 us
    pallas_call x1, Pallas kernels, column_stage(): pl.pallas_call(column_kernel, out_shape=jax.ShapeDtypeStruct((groups, 2,...  4.41 us
    pallas_call x1, Pallas kernels, final_stage(): pl.pallas_call(functools.partial(final_kernel, scale=scale), out_shape=ja...  3.42 us

profile of v6, /device:TPU:14, one launch (start us, length us, event | category | flops | bytes accessed | tf_op | source)
XLA Modules:
  0.0 102.9 jit_solution(10849027591940019141)
XLA Ops:
  0.0 0.7 constant_dynamic-slice_fusion
  0.7 1.8 %multiply_add_fusion = (f32[256,128]{1,0:T(8,128)}, f32[256,128]{1,0:T(8,128)}) fusion(f32[256,128]{1,0:T(8,128)} %constant.43.clone, f32[256,128]{1,0:T(8,128)} %constant.44.clone, f32[256]{0:T(256)S(1)} %bitcast.2, f32[256]{0:T(256)S(1)} %bitcast.3), kind=kLoop, calls=%fused_computation | loop fusion | flops 196608 | bytes 526336 | tf_op jit(solution)/shard_map/add | solution.py:282
  2.5 4.8 %shard_map.109 = f32[16,2,6,16,128]{4,3,2,1,0:T(8,128)} custom-call(s32[6,512,128]{2,1,0:T(8,128)} %limbs_ref.1, bf16[1024,512]{1,0:T(8,128)(2,1)} %constant.39.clone.matrix_ref, f32[256,128]{1,0:T(8,128)} %get-tuple-element.6.turn_cos_ref, f32[256,128]{1,0:T(8,128)} %get-tuple-element.5.turn_sin_ref), custom_call_target="tpu_custom_call" | custom-call | flops 1610612736 | bytes 5767168 | tf_op jit(solution)/shard_map/pallas_call | solution.py:80
  7.4 57.3 %all_to_all.10.in_ref = f32[16,2,6,16,128]{4,3,2,1,0:T(8,128)} all-to-all(f32[16,2,6,16,128]{4,3,2,1,0:T(8,128)} %shard_map.109), channel_id=1, replica_groups=mesh['pair'=32,'row'=2,'col'=8] {'row','col'}, dimensions={0} | all-to-all | bytes 3145728 | tf_op jit(solution)/shard_map/all_to_all | solution.py:286
  64.7 4.4 %shard_map.110 = f32[16,2,3,16,128]{4,3,2,1,0:T(8,128)} custom-call(f32[16,2,6,16,128]{4,3,2,1,0:T(8,128)} %all_to_all.10.in_ref, f32[16,128]{1,0:T(8,128)} %constant.45.clone.twist_cos_ref, f32[16,128]{1,0:T(8,128)} %constant.46.clone.twist_sin_ref, bf16[512,256]{1,0:T(8,128)(2,1)} %constant.47.clone.forward_ref, bf16[512,256]{1,0:T(8,128)(2,1)} %constant.48.clone.inverse_ref), custom_call_target="tpu_custom_call" | custom-call | flops 905969664 | bytes 2359296 | tf_op jit(solution)/shard_map/pallas_call | solution.py:239
  69.1 30.4 %all_to_all.11.pieces_ref = f32[16,2,3,16,128]{4,3,2,1,0:T(8,128)} all-to-all(f32[16,2,3,16,128]{4,3,2,1,0:T(8,128)} %shard_map.110), channel_id=1, replica_groups=mesh['pair'=32,'row'=2,'col'=8] {'row','col'}, dimensions={0} | all-to-all | bytes 1572864 | tf_op jit(solution)/shard_map/all_to_all | solution.py:303
  99.5 3.4 %shard_map.111 = f32[3,512,128]{2,1,0:T(8,128)} custom-call(f32[16,2,3,16,128]{4,3,2,1,0:T(8,128)} %all_to_all.11.pieces_ref, bf16[1024,512]{1,0:T(8,128)(2,1)} %constant.40.clone.matrix_ref, f32[256,128]{1,0:T(8,128)} %get-tuple-element.6.turn_cos_ref, f32[256,128]{1,0:T(8,128)} %get-tuple-element.5.turn_sin_ref), custom_call_target="tpu_custom_call" | custom-call | flops 1610612736 | bytes 3407872 | tf_op jit(solution)/shard_map/pallas_call | solution.py:126

commit v7 on v6

--- a/solution.py
+++ b/solution.py
@@ -271,8 +271,11 @@
     base_cos, base_sin = exact_phases(
         device_index[:, None] * narrow * (2 * half_index[None, :] + 1), limb_total
     )
-    base_cos = lax.dynamic_index_in_dim(constant(base_cos), device, 0, keepdims=False)[:, None]
-    base_sin = lax.dynamic_index_in_dim(constant(base_sin), device, 0, keepdims=False)[:, None]
+    chooser = (
+        lax.broadcasted_iota(jnp.int32, (groups, narrow), 0) == device
+    ).astype(jnp.float32)
+    base_cos = jnp.dot(constant(base_cos.T), chooser, precision=highest)
+    base_sin = jnp.dot(constant(base_sin.T), chooser, precision=highest)
     lane_index = np.arange(narrow, dtype=np.int64)
     lane_cos, lane_sin = exact_phases(lane_index[None, :] * (2 * half_index[:, None] + 1), limb_total)
     lane_cos = constant(lane_cos)

time: 103 us -> 104 us (level)
  the two profiles are of different devices: /device:TPU:14 before, /device:TPU:8 now
where the time goes in v7:
time: 104 us
  blocking collectives  87.7 us (84%)
  Pallas kernels  12.7 us (12%)
  matrix products  3.18 us (3%)
    all_to_all x1, blocking collectives, body(): received = lax.all_to_all(send, ('row', 'col'), 0, 0, tiled=True)  57.3 us
    all_to_all x1, blocking collectives, body(): pieces = lax.all_to_all(outgoing, ('row', 'col'), 0, 0, tiled=True)  30.4 us
    pallas_call x1, Pallas kernels, row_stage(): pl.pallas_call(row_kernel, out_shape=jax.ShapeDtypeStruct((groups, 2, num...  4.84 us
    pallas_call x1, Pallas kernels, column_stage(): pl.pallas_call(column_kernel, out_shape=jax.ShapeDtypeStruct((groups, 2,...  4.41 us
    pallas_call x1, Pallas kernels, final_stage(): pl.pallas_call(functools.partial(final_kernel, scale=scale), out_shape=ja...  3.42 us

profile of v7, /device:TPU:8, one launch (start us, length us, event | category | flops | bytes accessed | tf_op | source)
XLA Modules:
  0.0 103.6 jit_solution(10095735865232438930)
XLA Ops:
  0.0 1.2 %fusion.2 = f32[256,128]{1,0:T(8,128)S(1)} fusion(f32[256,16]{1,0:T(8,128)} %constant.33.clone, pred[16]{0:T(512)(128)(4,1)S(1)} %iota_compare_fusion), kind=kOutput, calls=%fused_computation.4 | convolution fusion | flops 6291456 | bytes 147472 | tf_op jit(solution)/shard_map/dot_general | solution.py:277
  1.2 2.0 %multiply_add_fusion = (f32[256,128]{1,0:T(8,128)}, f32[256,128]{1,0:T(8,128)}) fusion(f32[256,128]{1,0:T(8,128)} %constant.35.clone, f32[256,128]{1,0:T(8,128)S(1)} %fusion.2, f32[256,128]{1,0:T(8,128)} %constant.36.clone, f32[256,16]{1,0:T(8,128)} %constant.34.clone, pred[16]{0:T(512)(128)(4,1)S(1)} %iota_compare_fusion), kind=kOutput, calls=%fused_computation | convolution fusion | flops 6488064 | bytes 671760 | tf_op jit(solution)/shard_map/dot_general | solution.py:278
  3.2 4.8 %shard_map.109 = f32[16,2,6,16,128]{4,3,2,1,0:T(8,128)} custom-call(s32[6,512,128]{2,1,0:T(8,128)} %limbs_ref.1, bf16[1024,512]{1,0:T(8,128)(2,1)} %constant.31.clone.matrix_ref, f32[256,128]{1,0:T(8,128)} %get-tuple-element.6.turn_cos_ref, f32[256,128]{1,0:T(8,128)} %get-tuple-element.5.turn_sin_ref), custom_call_target="tpu_custom_call" | custom-call | flops 1610612736 | bytes 5767168 | tf_op jit(solution)/shard_map/pallas_call | solution.py:80
  8.0 57.3 %all_to_all.10.in_ref = f32[16,2,6,16,128]{4,3,2,1,0:T(8,128)} all-to-all(f32[16,2,6,16,128]{4,3,2,1,0:T(8,128)} %shard_map.109), channel_id=1, replica_groups=mesh['pair'=32,'row'=2,'col'=8] {'row','col'}, dimensions={0} | all-to-all | bytes 3145728 | tf_op jit(solution)/shard_map/all_to_all | solution.py:289
  65.4 4.4 %shard_map.110 = f32[16,2,3,16,128]{4,3,2,1,0:T(8,128)} custom-call(f32[16,2,6,16,128]{4,3,2,1,0:T(8,128)} %all_to_all.10.in_ref, f32[16,128]{1,0:T(8,128)} %constant.37.clone.twist_cos_ref, f32[16,128]{1,0:T(8,128)} %constant.38.clone.twist_sin_ref, bf16[512,256]{1,0:T(8,128)(2,1)} %constant.39.clone.forward_ref, bf16[512,256]{1,0:T(8,128)(2,1)} %constant.40.clone.inverse_ref), custom_call_target="tpu_custom_call" | custom-call | flops 905969664 | bytes 2359296 | tf_op jit(solution)/shard_map/pallas_call | solution.py:239
  69.8 30.4 %all_to_all.11.pieces_ref = f32[16,2,3,16,128]{4,3,2,1,0:T(8,128)} all-to-all(f32[16,2,3,16,128]{4,3,2,1,0:T(8,128)} %shard_map.110), channel_id=1, replica_groups=mesh['pair'=32,'row'=2,'col'=8] {'row','col'}, dimensions={0} | all-to-all | bytes 1572864 | tf_op jit(solution)/shard_map/all_to_all | solution.py:306
  100.2 3.4 %shard_map.111 = f32[3,512,128]{2,1,0:T(8,128)} custom-call(f32[16,2,3,16,128]{4,3,2,1,0:T(8,128)} %all_to_all.11.pieces_ref, bf16[1024,512]{1,0:T(8,128)(2,1)} %constant.32.clone.matrix_ref, f32[256,128]{1,0:T(8,128)} %get-tuple-element.6.turn_cos_ref, f32[256,128]{1,0:T(8,128)} %get-tuple-element.5.turn_sin_ref), custom_call_target="tpu_custom_call" | custom-call | flops 1610612736 | bytes 3407872 | tf_op jit(solution)/shard_map/pallas_call | solution.py:126
  (1 shorter events, 0.0 us)

commit v8 on v6

--- a/solution.py
+++ b/solution.py
@@ -47,11 +47,11 @@
     return ar * br - ai * bi, ar * bi + ai * br
 
 
-def row_kernel(limbs_ref, matrix_ref, turn_cos_ref, turn_sin_ref, out_ref):
+def row_kernel(limbs_ref, matrix_ref, chooser_ref, base_cos_ref, base_sin_ref, lane_cos_ref, lane_sin_ref, out_ref):
     number = limbs_ref.shape[0]
-    half = turn_cos_ref.shape[0]
+    half = lane_cos_ref.shape[0]
     groups, _, _, local, narrow = out_ref.shape
-    turn_cos, turn_sin = turn_tables(turn_cos_ref, turn_sin_ref)
+    turn_cos, turn_sin = turn_tables(chooser_ref, base_cos_ref, base_sin_ref, lane_cos_ref, lane_sin_ref)
     centred = [limbs_ref[i] - jnp.int32(32768) for i in range(number)]
     upper = [lax.shift_right_arithmetic(value, jnp.int32(8)) for value in centred]
     lower = [value - top * jnp.int32(256) for value, top in zip(centred, upper)]
@@ -69,13 +69,18 @@
         out_ref[:, 1, i] = (real_rows * turn_sin + imag_rows * turn_cos).reshape(groups, local, narrow)
 
 
-def turn_tables(turn_cos_ref, turn_sin_ref):
-    return turn_cos_ref[...], turn_sin_ref[...]
+def turn_tables(chooser_ref, base_cos_ref, base_sin_ref, lane_cos_ref, lane_sin_ref):
+    pick = chooser_ref[...]
+    base_cos = jnp.sum(base_cos_ref[...] * pick, axis=1, keepdims=True)
+    base_sin = jnp.sum(base_sin_ref[...] * pick, axis=1, keepdims=True)
+    lane_cos = lane_cos_ref[...]
+    lane_sin = lane_sin_ref[...]
+    return base_cos * lane_cos - base_sin * lane_sin, base_cos * lane_sin + base_sin * lane_cos
 
 
 def row_stage(limbs, matrix, tables, groups):
     number, height, narrow = limbs.shape
-    half = tables[0].shape[0]
+    half = tables[3].shape[0]
     local = half // groups
     return pl.pallas_call(
         row_kernel,
@@ -88,10 +93,10 @@
     )(limbs, matrix, *tables)
 
 
-def final_kernel(pieces_ref, matrix_ref, turn_cos_ref, turn_sin_ref, out_ref, *, scale):
+def final_kernel(pieces_ref, matrix_ref, chooser_ref, base_cos_ref, base_sin_ref, lane_cos_ref, lane_sin_ref, out_ref, *, scale):
     groups, _, outputs, local, narrow = pieces_ref.shape
     half = groups * local
-    turn_cos, turn_sin = turn_tables(turn_cos_ref, turn_sin_ref)
+    turn_cos, turn_sin = turn_tables(chooser_ref, base_cos_ref, base_sin_ref, lane_cos_ref, lane_sin_ref)
     turn_cos = turn_cos.reshape(groups, local, narrow)
     turn_sin = turn_sin.reshape(groups, local, narrow)
     columns = []
@@ -271,15 +276,19 @@
     base_cos, base_sin = exact_phases(
         device_index[:, None] * narrow * (2 * half_index[None, :] + 1), limb_total
     )
-    base_cos = lax.dynamic_index_in_dim(constant(base_cos), device, 0, keepdims=False)[:, None]
-    base_sin = lax.dynamic_index_in_dim(constant(base_sin), device, 0, keepdims=False)[:, None]
+    base_cos_table = np.zeros((half, narrow))
+    base_sin_table = np.zeros((half, narrow))
+    base_cos_table[:, :groups] = base_cos.T
+    base_sin_table[:, :groups] = base_sin.T
+    chooser = (lax.broadcasted_iota(jnp.int32, (1, narrow), 1) == device).astype(jnp.float32)
     lane_index = np.arange(narrow, dtype=np.int64)
     lane_cos, lane_sin = exact_phases(lane_index[None, :] * (2 * half_index[:, None] + 1), limb_total)
-    lane_cos = constant(lane_cos)
-    lane_sin = constant(lane_sin)
     tables = (
-        base_cos * lane_cos - base_sin * lane_sin,
-        base_cos * lane_sin + base_sin * lane_cos,
+        chooser,
+        constant(base_cos_table),
+        constant(base_sin_table),
+        constant(lane_cos),
+        constant(lane_sin),
     )
 
     send = row_stage(limbs, row_matrix, tables, groups)

time: 103 us -> 101 us (0.981)
  the two profiles are of different devices: /device:TPU:14 before, /device:TPU:12 now
where the time goes in v8:
time: 101 us
  blocking collectives  87.7 us (87%)
  Pallas kernels  13 us (13%)
    all_to_all x1, blocking collectives, body(): received = lax.all_to_all(send, ('row', 'col'), 0, 0, tiled=True)  57.3 us
    all_to_all x1, blocking collectives, body(): pieces = lax.all_to_all(outgoing, ('row', 'col'), 0, 0, tiled=True)  30.4 us
    pallas_call x1, Pallas kernels, row_stage(): pl.pallas_call(row_kernel, out_shape=jax.ShapeDtypeStruct((groups, 2, num...  4.96 us
    pallas_call x1, Pallas kernels, column_stage(): pl.pallas_call(column_kernel, out_shape=jax.ShapeDtypeStruct((groups, 2,...  4.41 us
    pallas_call x1, Pallas kernels, final_stage(): pl.pallas_call(functools.partial(final_kernel, scale=scale), out_shape=ja...  3.62 us

profile of v8, /device:TPU:12, one launch (start us, length us, event | category | flops | bytes accessed | tf_op | source)
XLA Modules:
  0.0 101.2 jit_solution(6033506434668033958)
XLA Ops:
  0.0 0.5 compare_convert_fusion.chooser_ref
  0.5 5.0 %shard_map.109 = f32[16,2,6,16,128]{4,3,2,1,0:T(8,128)} custom-call(s32[6,512,128]{2,1,0:T(8,128)} %limbs_ref.1, bf16[1024,512]{1,0:T(8,128)(2,1)} %constant.31.clone.matrix_ref, f32[1,128]{1,0:T(1,128)} %compare_convert_fusion.chooser_ref, f32[256,128]{1,0:T(8,128)} %constant.33.clone.base_cos_ref, f32[256,128]{1,0:T(8,128)} %constant.34.clone.base_sin_ref, ...), custom_call_target="tpu_custom_call" | custom-call | flops 1610612736 | bytes 5767168 | tf_op jit(solution)/shard_map/pallas_call | solution.py:85
  5.4 57.3 %all_to_all.10.in_ref = f32[16,2,6,16,128]{4,3,2,1,0:T(8,128)} all-to-all(f32[16,2,6,16,128]{4,3,2,1,0:T(8,128)} %shard_map.109), channel_id=1, replica_groups=mesh['pair'=32,'row'=2,'col'=8] {'row','col'}, dimensions={0} | all-to-all | bytes 3145728 | tf_op jit(solution)/shard_map/all_to_all | solution.py:295
  62.8 4.4 %shard_map.110 = f32[16,2,3,16,128]{4,3,2,1,0:T(8,128)} custom-call(f32[16,2,6,16,128]{4,3,2,1,0:T(8,128)} %all_to_all.10.in_ref, f32[16,128]{1,0:T(8,128)} %constant.37.clone.twist_cos_ref, f32[16,128]{1,0:T(8,128)} %constant.38.clone.twist_sin_ref, bf16[512,256]{1,0:T(8,128)(2,1)} %constant.39.clone.forward_ref, bf16[512,256]{1,0:T(8,128)(2,1)} %constant.40.clone.inverse_ref), custom_call_target="tpu_custom_call" | custom-call | flops 905969664 | bytes 2359296 | tf_op jit(solution)/shard_map/pallas_call | solution.py:244
  67.2 30.4 %all_to_all.11.pieces_ref = f32[16,2,3,16,128]{4,3,2,1,0:T(8,128)} all-to-all(f32[16,2,3,16,128]{4,3,2,1,0:T(8,128)} %shard_map.110), channel_id=1, replica_groups=mesh['pair'=32,'row'=2,'col'=8] {'row','col'}, dimensions={0} | all-to-all | bytes 1572864 | tf_op jit(solution)/shard_map/all_to_all | solution.py:312
  97.6 3.6 %shard_map.111 = f32[3,512,128]{2,1,0:T(8,128)} custom-call(f32[16,2,3,16,128]{4,3,2,1,0:T(8,128)} %all_to_all.11.pieces_ref, bf16[1024,512]{1,0:T(8,128)(2,1)} %constant.32.clone.matrix_ref, f32[1,128]{1,0:T(1,128)} %compare_convert_fusion.chooser_ref, f32[256,128]{1,0:T(8,128)} %constant.33.clone.base_cos_ref, f32[256,128]{1,0:T(8,128)} %constant.34.clone.base_sin_ref, ...), custom_call_target="tpu_custom_call" | custom-call | flops 1610612736 | bytes 3407872 | tf_op jit(solution)/shard_map/pallas_call | solution.py:131

commit v9 on v8

--- a/solution.py
+++ b/solution.py
@@ -82,9 +82,16 @@
     number, height, narrow = limbs.shape
     half = tables[3].shape[0]
     local = half // groups
+    steps = 2
+    block = number // steps
+    fixed = lambda shape: pl.BlockSpec(shape, lambda s: (0,) * len(shape))
     return pl.pallas_call(
         row_kernel,
         out_shape=jax.ShapeDtypeStruct((groups, 2, number, local, narrow), jnp.float32),
+        grid=(steps,),
+        in_specs=[pl.BlockSpec((block, height, narrow), lambda s: (s, 0, 0)), fixed(matrix.shape)]
+        + [fixed(table.shape) for table in tables],
+        out_specs=pl.BlockSpec((groups, 2, block, local, narrow), lambda s: (0, 0, s, 0, 0)),
         cost_estimate=pl.CostEstimate(
             flops=2 * 4 * half * height * 2 * narrow * number,
             transcendentals=0,
@@ -128,9 +135,14 @@
 def final_stage(pieces, matrix, tables, scale):
     groups, _, outputs, local, narrow = pieces.shape
     height = matrix.shape[0] // 2
+    fixed = lambda shape: pl.BlockSpec(shape, lambda s: (0,) * len(shape))
     return pl.pallas_call(
         functools.partial(final_kernel, scale=scale),
         out_shape=jax.ShapeDtypeStruct((outputs, height, narrow), jnp.float32),
+        grid=(outputs,),
+        in_specs=[pl.BlockSpec((groups, 2, 1, local, narrow), lambda s: (0, 0, s, 0, 0)), fixed(matrix.shape)]
+        + [fixed(table.shape) for table in tables],
+        out_specs=pl.BlockSpec((1, height, narrow), lambda s: (s, 0, 0)),
         cost_estimate=pl.CostEstimate(
             flops=2 * 4 * height * height * 2 * outputs * narrow,
             transcendentals=0,

time: 101 us -> 102 us (level)
  the two profiles are of different devices: /device:TPU:12 before, /device:TPU:14 now
where the time goes in v9:
time: 102 us
  blocking collectives  87.8 us (86%)
  Pallas kernels  13.5 us (13%)
    all_to_all x1, blocking collectives, body(): received = lax.all_to_all(send, ('row', 'col'), 0, 0, tiled=True)  57.4 us
    all_to_all x1, blocking collectives, body(): pieces = lax.all_to_all(outgoing, ('row', 'col'), 0, 0, tiled=True)  30.4 us
    pallas_call x1, Pallas kernels, row_stage(): pl.pallas_call(row_kernel, out_shape=jax.ShapeDtypeStruct((groups, 2, num...  4.73 us
    pallas_call x1, Pallas kernels, column_stage(): pl.pallas_call(column_kernel, out_shape=jax.ShapeDtypeStruct((groups, 2,...  4.41 us
    pallas_call x1, Pallas kernels, final_stage(): pl.pallas_call(functools.partial(final_kernel, scale=scale), out_shape=ja...  4.32 us

profile of v9, /device:TPU:14, one launch (start us, length us, event | category | flops | bytes accessed | tf_op | source)
XLA Modules:
  0.0 101.8 jit_solution(8395872838279677164)
XLA Ops:
  0.0 0.5 compare_convert_fusion.chooser_ref
  0.5 4.7 %shard_map.109 = f32[16,2,6,16,128]{4,3,2,1,0:T(8,128)} custom-call(s32[6,512,128]{2,1,0:T(8,128)} %limbs_ref.1, bf16[1024,512]{1,0:T(8,128)(2,1)} %constant.31.clone.matrix_ref, f32[1,128]{1,0:T(1,128)} %compare_convert_fusion.chooser_ref, f32[256,128]{1,0:T(8,128)} %constant.33.clone.base_cos_ref, f32[256,128]{1,0:T(8,128)} %constant.34.clone.base_sin_ref, ...), custom_call_target="tpu_custom_call" | custom-call | flops 1610612736 | bytes 5767168 | tf_op jit(solution)/shard_map/pallas_call | solution.py:88
  5.2 57.4 %all_to_all.10.in_ref = f32[16,2,6,16,128]{4,3,2,1,0:T(8,128)} all-to-all(f32[16,2,6,16,128]{4,3,2,1,0:T(8,128)} %shard_map.109), channel_id=1, replica_groups=mesh['pair'=32,'row'=2,'col'=8] {'row','col'}, dimensions={0} | all-to-all | bytes 3145728 | tf_op jit(solution)/shard_map/all_to_all | solution.py:307
  62.6 4.4 %shard_map.110 = f32[16,2,3,16,128]{4,3,2,1,0:T(8,128)} custom-call(f32[16,2,6,16,128]{4,3,2,1,0:T(8,128)} %all_to_all.10.in_ref, f32[16,128]{1,0:T(8,128)} %constant.37.clone.twist_cos_ref, f32[16,128]{1,0:T(8,128)} %constant.38.clone.twist_sin_ref, bf16[512,256]{1,0:T(8,128)(2,1)} %constant.39.clone.forward_ref, bf16[512,256]{1,0:T(8,128)(2,1)} %constant.40.clone.inverse_ref), custom_call_target="tpu_custom_call" | custom-call | flops 905969664 | bytes 2359296 | tf_op jit(solution)/shard_map/pallas_call | solution.py:256
  67.0 30.4 %all_to_all.11.pieces_ref = f32[16,2,3,16,128]{4,3,2,1,0:T(8,128)} all-to-all(f32[16,2,3,16,128]{4,3,2,1,0:T(8,128)} %shard_map.110), channel_id=1, replica_groups=mesh['pair'=32,'row'=2,'col'=8] {'row','col'}, dimensions={0} | all-to-all | bytes 1572864 | tf_op jit(solution)/shard_map/all_to_all | solution.py:324
  97.4 4.3 %shard_map.111 = f32[3,512,128]{2,1,0:T(8,128)} custom-call(f32[16,2,3,16,128]{4,3,2,1,0:T(8,128)} %all_to_all.11.pieces_ref, bf16[1024,512]{1,0:T(8,128)(2,1)} %constant.32.clone.matrix_ref, f32[1,128]{1,0:T(1,128)} %compare_convert_fusion.chooser_ref, f32[256,128]{1,0:T(8,128)} %constant.33.clone.base_cos_ref, f32[256,128]{1,0:T(8,128)} %constant.34.clone.base_sin_ref, ...), custom_call_target="tpu_custom_call" | custom-call | flops 1610612736 | bytes 3407872 | tf_op jit(solution)/shard_map/pallas_call | solution.py:139

commit v10 on v9

--- a/solution.py
+++ b/solution.py
@@ -47,11 +47,11 @@
     return ar * br - ai * bi, ar * bi + ai * br
 
 
-def row_kernel(limbs_ref, matrix_ref, chooser_ref, base_cos_ref, base_sin_ref, lane_cos_ref, lane_sin_ref, out_ref):
+def row_kernel(limbs_ref, matrix_ref, base_cos_ref, base_sin_ref, lane_cos_ref, lane_sin_ref, out_ref):
     number = limbs_ref.shape[0]
     half = lane_cos_ref.shape[0]
     groups, _, _, local, narrow = out_ref.shape
-    turn_cos, turn_sin = turn_tables(chooser_ref, base_cos_ref, base_sin_ref, lane_cos_ref, lane_sin_ref)
+    turn_cos, turn_sin = turn_tables(base_cos_ref, base_sin_ref, lane_cos_ref, lane_sin_ref)
     centred = [limbs_ref[i] - jnp.int32(32768) for i in range(number)]
     upper = [lax.shift_right_arithmetic(value, jnp.int32(8)) for value in centred]
     lower = [value - top * jnp.int32(256) for value, top in zip(centred, upper)]
@@ -69,8 +69,9 @@
         out_ref[:, 1, i] = (real_rows * turn_sin + imag_rows * turn_cos).reshape(groups, local, narrow)
 
 
-def turn_tables(chooser_ref, base_cos_ref, base_sin_ref, lane_cos_ref, lane_sin_ref):
-    pick = chooser_ref[...]
+def turn_tables(base_cos_ref, base_sin_ref, lane_cos_ref, lane_sin_ref):
+    device = lax.axis_index("row") * lax.axis_size("col") + lax.axis_index("col")
+    pick = (lax.broadcasted_iota(jnp.int32, (1, base_cos_ref.shape[1]), 1) == device).astype(jnp.float32)
     base_cos = jnp.sum(base_cos_ref[...] * pick, axis=1, keepdims=True)
     base_sin = jnp.sum(base_sin_ref[...] * pick, axis=1, keepdims=True)
     lane_cos = lane_cos_ref[...]
@@ -80,7 +81,7 @@
 
 def row_stage(limbs, matrix, tables, groups):
     number, height, narrow = limbs.shape
-    half = tables[3].shape[0]
+    half = tables[2].shape[0]
     local = half // groups
     steps = 2
     block = number // steps
@@ -100,10 +101,10 @@
     )(limbs, matrix, *tables)
 
 
-def final_kernel(pieces_ref, matrix_ref, chooser_ref, base_cos_ref, base_sin_ref, lane_cos_ref, lane_sin_ref, out_ref, *, scale):
+def final_kernel(pieces_ref, matrix_ref, base_cos_ref, base_sin_ref, lane_cos_ref, lane_sin_ref, out_ref, *, scale):
     groups, _, outputs, local, narrow = pieces_ref.shape
     half = groups * local
-    turn_cos, turn_sin = turn_tables(chooser_ref, base_cos_ref, base_sin_ref, lane_cos_ref, lane_sin_ref)
+    turn_cos, turn_sin = turn_tables(base_cos_ref, base_sin_ref, lane_cos_ref, lane_sin_ref)
     turn_cos = turn_cos.reshape(groups, local, narrow)
     turn_sin = turn_sin.reshape(groups, local, narrow)
     columns = []
@@ -135,14 +136,9 @@
 def final_stage(pieces, matrix, tables, scale):
     groups, _, outputs, local, narrow = pieces.shape
     height = matrix.shape[0] // 2
-    fixed = lambda shape: pl.BlockSpec(shape, lambda s: (0,) * len(shape))
     return pl.pallas_call(
         functools.partial(final_kernel, scale=scale),
         out_shape=jax.ShapeDtypeStruct((outputs, height, narrow), jnp.float32),
-        grid=(outputs,),
-        in_specs=[pl.BlockSpec((groups, 2, 1, local, narrow), lambda s: (0, 0, s, 0, 0)), fixed(matrix.shape)]
-        + [fixed(table.shape) for table in tables],
-        out_specs=pl.BlockSpec((1, height, narrow), lambda s: (s, 0, 0)),
         cost_estimate=pl.CostEstimate(
             flops=2 * 4 * height * height * 2 * outputs * narrow,
             transcendentals=0,
@@ -292,11 +288,9 @@
     base_sin_table = np.zeros((half, narrow))
     base_cos_table[:, :groups] = base_cos.T
     base_sin_table[:, :groups] = base_sin.T
-    chooser = (lax.broadcasted_iota(jnp.int32, (1, narrow), 1) == device).astype(jnp.float32)
     lane_index = np.arange(narrow, dtype=np.int64)
     lane_cos, lane_sin = exact_phases(lane_index[None, :] * (2 * half_index[:, None] + 1), limb_total)
     tables = (
-        chooser,
         constant(base_cos_table),
         constant(base_sin_table),
         constant(lane_cos),

time: 102 us -> 101 us (level)
  no operation moved by 1% of the time
where the time goes in v10:
time: 101 us
  blocking collectives  87.8 us (87%)
  Pallas kernels  12.8 us (13%)
    all_to_all x1, blocking collectives, body(): received = lax.all_to_all(send, ('row', 'col'), 0, 0, tiled=True)  57.4 us
    all_to_all x1, blocking collectives, body(): pieces = lax.all_to_all(outgoing, ('row', 'col'), 0, 0, tiled=True)  30.4 us
    pallas_call x1, Pallas kernels, row_stage(): pl.pallas_call(row_kernel, out_shape=jax.ShapeDtypeStruct((groups, 2, num...  4.72 us
    pallas_call x1, Pallas kernels, column_stage(): pl.pallas_call(column_kernel, out_shape=jax.ShapeDtypeStruct((groups, 2,...  4.41 us
    pallas_call x1, Pallas kernels, final_stage(): pl.pallas_call(functools.partial(final_kernel, scale=scale), out_shape=ja...  3.62 us

profile of v10, /device:TPU:14, one launch (start us, length us, event | category | flops | bytes accessed | tf_op | source)
XLA Modules:
  0.0 100.6 jit_solution(6038782671814878836)
XLA Ops:
  0.0 4.7 %shard_map.109 = f32[16,2,6,16,128]{4,3,2,1,0:T(8,128)} custom-call(s32[6,512,128]{2,1,0:T(8,128)} %limbs_ref.1, bf16[1024,512]{1,0:T(8,128)(2,1)} %constant.20.clone.matrix_ref, f32[256,128]{1,0:T(8,128)} %constant.22.clone.base_cos_ref, f32[256,128]{1,0:T(8,128)} %constant.23.clone.base_sin_ref, f32[256,128]{1,0:T(8,128)} %constant.24.clone.lane_cos_ref, ...), custom_call_target="tpu_custom_call" | custom-call | flops 1610612736 | bytes 5767168 | tf_op jit(solution)/shard_map/pallas_call | solution.py:89
  4.7 57.4 %all_to_all.10.in_ref = f32[16,2,6,16,128]{4,3,2,1,0:T(8,128)} all-to-all(f32[16,2,6,16,128]{4,3,2,1,0:T(8,128)} %shard_map.109), channel_id=1, replica_groups=mesh['pair'=32,'row'=2,'col'=8] {'row','col'}, dimensions={0} | all-to-all | bytes 3145728 | tf_op jit(solution)/shard_map/all_to_all | solution.py:301
  62.1 4.4 %shard_map.110 = f32[16,2,3,16,128]{4,3,2,1,0:T(8,128)} custom-call(f32[16,2,6,16,128]{4,3,2,1,0:T(8,128)} %all_to_all.10.in_ref, f32[16,128]{1,0:T(8,128)} %constant.26.clone.twist_cos_ref, f32[16,128]{1,0:T(8,128)} %constant.27.clone.twist_sin_ref, bf16[512,256]{1,0:T(8,128)(2,1)} %constant.28.clone.forward_ref, bf16[512,256]{1,0:T(8,128)(2,1)} %constant.29.clone.inverse_ref), custom_call_target="tpu_custom_call" | custom-call | flops 905969664 | bytes 2359296 | tf_op jit(solution)/shard_map/pallas_call | solution.py:252
  66.5 30.4 %all_to_all.11.pieces_ref = f32[16,2,3,16,128]{4,3,2,1,0:T(8,128)} all-to-all(f32[16,2,3,16,128]{4,3,2,1,0:T(8,128)} %shard_map.110), channel_id=1, replica_groups=mesh['pair'=32,'row'=2,'col'=8] {'row','col'}, dimensions={0} | all-to-all | bytes 1572864 | tf_op jit(solution)/shard_map/all_to_all | solution.py:318
  96.9 3.6 %shard_map.111 = f32[3,512,128]{2,1,0:T(8,128)} custom-call(f32[16,2,3,16,128]{4,3,2,1,0:T(8,128)} %all_to_all.11.pieces_ref, bf16[1024,512]{1,0:T(8,128)(2,1)} %constant.21.clone.matrix_ref, f32[256,128]{1,0:T(8,128)} %constant.22.clone.base_cos_ref, f32[256,128]{1,0:T(8,128)} %constant.23.clone.base_sin_ref, f32[256,128]{1,0:T(8,128)} %constant.24.clone.lane_cos_ref, ...), custom_call_target="tpu_custom_call" | custom-call | flops 1610612736 | bytes 3407872 | tf_op jit(solution)/shard_map/pallas_call | solution.py:139

commit v11 on v10

--- a/solution.py
+++ b/solution.py
@@ -33,6 +33,12 @@
     return constant(table_cos), constant(table_sin)
 
 
+def split_bf16_side(table):
+    first = table.astype(ml_dtypes.bfloat16)
+    second = (table - first.astype(np.float64)).astype(ml_dtypes.bfloat16)
+    return np.concatenate((first, second), axis=1)
+
+
 def split_bf16(table):
     first = table.astype(ml_dtypes.bfloat16)
     second = (table - first.astype(np.float64)).astype(ml_dtypes.bfloat16)
@@ -55,13 +61,14 @@
     centred = [limbs_ref[i] - jnp.int32(32768) for i in range(number)]
     upper = [lax.shift_right_arithmetic(value, jnp.int32(8)) for value in centred]
     lower = [value - top * jnp.int32(256) for value, top in zip(centred, upper)]
-    pieces = jnp.concatenate(upper + lower, axis=1).astype(jnp.float32).astype(jnp.bfloat16)
-    products = jnp.dot(matrix_ref[...], pieces, preferred_element_type=jnp.float32)
-    count = 2 * half
-    width = number * narrow
-    upper_part = products[:count, :width] + products[count:, :width]
-    lower_part = products[:count, width:] + products[count:, width:]
-    rows = (upper_part * 256.0 + lower_part) * (1.0 / 32768.0)
+    upper = jnp.concatenate(upper, axis=1).astype(jnp.float32) * 256.0
+    lower = jnp.concatenate(lower, axis=1).astype(jnp.float32)
+    upper = upper.astype(jnp.bfloat16)
+    lower = lower.astype(jnp.bfloat16)
+    matrix = matrix_ref[...]
+    rows = jnp.dot(matrix, jnp.concatenate((upper, upper), axis=0), preferred_element_type=jnp.float32)
+    rows = rows + jnp.dot(matrix, jnp.concatenate((lower, lower), axis=0), preferred_element_type=jnp.float32)
+    rows = rows * (1.0 / 32768.0)
     for i in range(number):
         real_rows = rows[:half, i * narrow : (i + 1) * narrow]
         imag_rows = rows[half:, i * narrow : (i + 1) * narrow]
@@ -122,20 +129,17 @@
     gathered = jnp.concatenate(columns, axis=1)
     first = gathered.astype(jnp.bfloat16)
     second = (gathered - first.astype(jnp.float32)).astype(jnp.bfloat16)
-    products = jnp.dot(
-        matrix_ref[...], jnp.concatenate((first, second), axis=1), preferred_element_type=jnp.float32
-    )
-    height = matrix_ref.shape[0] // 2
-    width = outputs * narrow
-    small = products[height:, width:] + products[height:, :width] + products[:height, width:]
-    total = (small + products[:height, :width]) * scale
+    matrix = matrix_ref[...]
+    small = jnp.dot(matrix, jnp.concatenate((second, second), axis=0), preferred_element_type=jnp.float32)
+    large = jnp.dot(matrix, jnp.concatenate((first, first), axis=0), preferred_element_type=jnp.float32)
+    total = (small + large) * scale
     for i in range(outputs):
         out_ref[i] = total[:, i * narrow : (i + 1) * narrow]
 
 
 def final_stage(pieces, matrix, tables, scale):
     groups, _, outputs, local, narrow = pieces.shape
-    height = matrix.shape[0] // 2
+    height = matrix.shape[0]
     return pl.pallas_call(
         functools.partial(final_kernel, scale=scale),
         out_shape=jax.ShapeDtypeStruct((outputs, height, narrow), jnp.float32),
@@ -278,8 +282,8 @@
     row_cos_exact, row_sin_exact = exact_phases(
         row_index[None, :] * (2 * half_index[:, None] + 1) % (2 * height), height
     )
-    row_matrix = jnp.asarray(split_bf16(np.concatenate((row_cos_exact, row_sin_exact), axis=0)))
-    final_matrix = jnp.asarray(split_bf16(np.concatenate((row_cos_exact, row_sin_exact), axis=0).T))
+    row_matrix = jnp.asarray(split_bf16_side(np.concatenate((row_cos_exact, row_sin_exact), axis=0)))
+    final_matrix = jnp.asarray(split_bf16_side(np.concatenate((row_cos_exact, row_sin_exact), axis=0).T))
     device_index = np.arange(groups, dtype=np.int64)
     base_cos, base_sin = exact_phases(
         device_index[:, None] * narrow * (2 * half_index[None, :] + 1), limb_total

time: 101 us -> 101 us (level)
  no operation moved by 1% of the time
where the time goes in v11:
time: 101 us
  blocking collectives  87.7 us (87%)
  Pallas kernels  13.4 us (13%)
    all_to_all x1, blocking collectives, body(): received = lax.all_to_all(send, ('row', 'col'), 0, 0, tiled=True)  57.3 us
    all_to_all x1, blocking collectives, body(): pieces = lax.all_to_all(outgoing, ('row', 'col'), 0, 0, tiled=True)  30.4 us
    pallas_call x1, Pallas kernels, row_stage(): pl.pallas_call(row_kernel, out_shape=jax.ShapeDtypeStruct((groups, 2, num...  5.17 us
    pallas_call x1, Pallas kernels, column_stage(): pl.pallas_call(column_kernel, out_shape=jax.ShapeDtypeStruct((groups, 2,...  4.41 us
    pallas_call x1, Pallas kernels, final_stage(): pl.pallas_call(functools.partial(final_kernel, scale=scale), out_shape=ja...  3.85 us

profile of v11, /device:TPU:14, one launch (start us, length us, event | category | flops | bytes accessed | tf_op | source)
XLA Modules:
  0.0 101.2 jit_solution(8761974031481330520)
XLA Ops:
  0.0 5.2 %shard_map.109 = f32[16,2,6,16,128]{4,3,2,1,0:T(8,128)} custom-call(s32[6,512,128]{2,1,0:T(8,128)} %limbs_ref.1, bf16[512,1024]{1,0:T(8,128)(2,1)} %constant.20.clone.matrix_ref, f32[256,128]{1,0:T(8,128)} %constant.22.clone.base_cos_ref, f32[256,128]{1,0:T(8,128)} %constant.23.clone.base_sin_ref, f32[256,128]{1,0:T(8,128)} %constant.24.clone.lane_cos_ref, ...), custom_call_target="tpu_custom_call" | custom-call | flops 1610612736 | bytes 5767168 | tf_op jit(solution)/shard_map/pallas_call | solution.py:96
  5.2 57.3 %all_to_all.10.in_ref = f32[16,2,6,16,128]{4,3,2,1,0:T(8,128)} all-to-all(f32[16,2,6,16,128]{4,3,2,1,0:T(8,128)} %shard_map.109), channel_id=1, replica_groups=mesh['pair'=32,'row'=2,'col'=8] {'row','col'}, dimensions={0} | all-to-all | bytes 3145728 | tf_op jit(solution)/shard_map/all_to_all | solution.py:305
  62.5 4.4 %shard_map.110 = f32[16,2,3,16,128]{4,3,2,1,0:T(8,128)} custom-call(f32[16,2,6,16,128]{4,3,2,1,0:T(8,128)} %all_to_all.10.in_ref, f32[16,128]{1,0:T(8,128)} %constant.26.clone.twist_cos_ref, f32[16,128]{1,0:T(8,128)} %constant.27.clone.twist_sin_ref, bf16[512,256]{1,0:T(8,128)(2,1)} %constant.28.clone.forward_ref, bf16[512,256]{1,0:T(8,128)(2,1)} %constant.29.clone.inverse_ref), custom_call_target="tpu_custom_call" | custom-call | flops 905969664 | bytes 2359296 | tf_op jit(solution)/shard_map/pallas_call | solution.py:256
  66.9 30.4 %all_to_all.11.pieces_ref = f32[16,2,3,16,128]{4,3,2,1,0:T(8,128)} all-to-all(f32[16,2,3,16,128]{4,3,2,1,0:T(8,128)} %shard_map.110), channel_id=1, replica_groups=mesh['pair'=32,'row'=2,'col'=8] {'row','col'}, dimensions={0} | all-to-all | bytes 1572864 | tf_op jit(solution)/shard_map/all_to_all | solution.py:322
  97.3 3.9 %shard_map.111 = f32[3,512,128]{2,1,0:T(8,128)} custom-call(f32[16,2,3,16,128]{4,3,2,1,0:T(8,128)} %all_to_all.11.pieces_ref, bf16[512,1024]{1,0:T(8,128)(2,1)} %constant.21.clone.matrix_ref, f32[256,128]{1,0:T(8,128)} %constant.22.clone.base_cos_ref, f32[256,128]{1,0:T(8,128)} %constant.23.clone.base_sin_ref, f32[256,128]{1,0:T(8,128)} %constant.24.clone.lane_cos_ref, ...), custom_call_target="tpu_custom_call" | custom-call | flops 1610612736 | bytes 3407872 | tf_op jit(solution)/shard_map/pallas_call | solution.py:143

commit v12 on v10

--- a/solution.py
+++ b/solution.py
@@ -83,7 +83,7 @@
     number, height, narrow = limbs.shape
     half = tables[2].shape[0]
     local = half // groups
-    steps = 2
+    steps = 3
     block = number // steps
     fixed = lambda shape: pl.BlockSpec(shape, lambda s: (0,) * len(shape))
     return pl.pallas_call(

time: 101 us -> 101 us (level)
  the two profiles are of different devices: /device:TPU:14 before, /device:TPU:12 now
where the time goes in v12:
time: 101 us
  blocking collectives  87.7 us (87%)
  Pallas kernels  13.1 us (13%)
    all_to_all x1, blocking collectives, body(): received = lax.all_to_all(send, ('row', 'col'), 0, 0, tiled=True)  57.3 us
    all_to_all x1, blocking collectives, body(): pieces = lax.all_to_all(outgoing, ('row', 'col'), 0, 0, tiled=True)  30.4 us
    pallas_call x1, Pallas kernels, row_stage(): pl.pallas_call(row_kernel, out_shape=jax.ShapeDtypeStruct((groups, 2, num...  5.1 us
    pallas_call x1, Pallas kernels, column_stage(): pl.pallas_call(column_kernel, out_shape=jax.ShapeDtypeStruct((groups, 2,...  4.41 us
    pallas_call x1, Pallas kernels, final_stage(): pl.pallas_call(functools.partial(final_kernel, scale=scale), out_shape=ja...  3.62 us

profile of v12, /device:TPU:12, one launch (start us, length us, event | category | flops | bytes accessed | tf_op | source)
XLA Modules:
  0.0 100.8 jit_solution(4667161249668919986)
XLA Ops:
  0.0 5.1 %shard_map.109 = f32[16,2,6,16,128]{4,3,2,1,0:T(8,128)} custom-call(s32[6,512,128]{2,1,0:T(8,128)} %limbs_ref.1, bf16[1024,512]{1,0:T(8,128)(2,1)} %constant.20.clone.matrix_ref, f32[256,128]{1,0:T(8,128)} %constant.22.clone.base_cos_ref, f32[256,128]{1,0:T(8,128)} %constant.23.clone.base_sin_ref, f32[256,128]{1,0:T(8,128)} %constant.24.clone.lane_cos_ref, ...), custom_call_target="tpu_custom_call" | custom-call | flops 1610612736 | bytes 5767168 | tf_op jit(solution)/shard_map/pallas_call | solution.py:89
  5.1 57.3 %all_to_all.10.in_ref = f32[16,2,6,16,128]{4,3,2,1,0:T(8,128)} all-to-all(f32[16,2,6,16,128]{4,3,2,1,0:T(8,128)} %shard_map.109), channel_id=1, replica_groups=mesh['pair'=32,'row'=2,'col'=8] {'row','col'}, dimensions={0} | all-to-all | bytes 3145728 | tf_op jit(solution)/shard_map/all_to_all | solution.py:301
  62.4 4.4 %shard_map.110 = f32[16,2,3,16,128]{4,3,2,1,0:T(8,128)} custom-call(f32[16,2,6,16,128]{4,3,2,1,0:T(8,128)} %all_to_all.10.in_ref, f32[16,128]{1,0:T(8,128)} %constant.26.clone.twist_cos_ref, f32[16,128]{1,0:T(8,128)} %constant.27.clone.twist_sin_ref, bf16[512,256]{1,0:T(8,128)(2,1)} %constant.28.clone.forward_ref, bf16[512,256]{1,0:T(8,128)(2,1)} %constant.29.clone.inverse_ref), custom_call_target="tpu_custom_call" | custom-call | flops 905969664 | bytes 2359296 | tf_op jit(solution)/shard_map/pallas_call | solution.py:252
  66.9 30.4 %all_to_all.11.pieces_ref = f32[16,2,3,16,128]{4,3,2,1,0:T(8,128)} all-to-all(f32[16,2,3,16,128]{4,3,2,1,0:T(8,128)} %shard_map.110), channel_id=1, replica_groups=mesh['pair'=32,'row'=2,'col'=8] {'row','col'}, dimensions={0} | all-to-all | bytes 1572864 | tf_op jit(solution)/shard_map/all_to_all | solution.py:318
  97.2 3.6 %shard_map.111 = f32[3,512,128]{2,1,0:T(8,128)} custom-call(f32[16,2,3,16,128]{4,3,2,1,0:T(8,128)} %all_to_all.11.pieces_ref, bf16[1024,512]{1,0:T(8,128)(2,1)} %constant.21.clone.matrix_ref, f32[256,128]{1,0:T(8,128)} %constant.22.clone.base_cos_ref, f32[256,128]{1,0:T(8,128)} %constant.23.clone.base_sin_ref, f32[256,128]{1,0:T(8,128)} %constant.24.clone.lane_cos_ref, ...), custom_call_target="tpu_custom_call" | custom-call | flops 1610612736 | bytes 3407872 | tf_op jit(solution)/shard_map/pallas_call | solution.py:139

commit v13 on v10

--- a/solution.py
+++ b/solution.py
@@ -122,13 +122,14 @@
     gathered = jnp.concatenate(columns, axis=1)
     first = gathered.astype(jnp.bfloat16)
     second = (gathered - first.astype(jnp.float32)).astype(jnp.bfloat16)
-    products = jnp.dot(
-        matrix_ref[...], jnp.concatenate((first, second), axis=1), preferred_element_type=jnp.float32
-    )
     height = matrix_ref.shape[0] // 2
     width = outputs * narrow
-    small = products[height:, width:] + products[height:, :width] + products[:height, width:]
-    total = (small + products[:height, :width]) * scale
+    leading = jnp.dot(
+        matrix_ref[:height], jnp.concatenate((first, second), axis=1), preferred_element_type=jnp.float32
+    )
+    trailing = jnp.dot(matrix_ref[height:], first, preferred_element_type=jnp.float32)
+    small = trailing + leading[:, width:]
+    total = (small + leading[:, :width]) * scale
     for i in range(outputs):
         out_ref[i] = total[:, i * narrow : (i + 1) * narrow]
 
@@ -140,7 +141,7 @@
         functools.partial(final_kernel, scale=scale),
         out_shape=jax.ShapeDtypeStruct((outputs, height, narrow), jnp.float32),
         cost_estimate=pl.CostEstimate(
-            flops=2 * 4 * height * height * 2 * outputs * narrow,
+            flops=2 * 3 * height * height * 2 * outputs * narrow,
             transcendentals=0,
             bytes_accessed=4 * 3 * outputs * height * narrow + 2 * 2 * height * height,
         ),

time: 101 us -> 101 us (level)
  no operation moved by 1% of the time
where the time goes in v13:
time: 101 us; the launch traced here: 100 us
  blocking collectives  87.8 us (87%)
  Pallas kernels  12.6 us (12%)
    all_to_all x1, blocking collectives, body(): received = lax.all_to_all(send, ('row', 'col'), 0, 0, tiled=True)  57.4 us
    all_to_all x1, blocking collectives, body(): pieces = lax.all_to_all(outgoing, ('row', 'col'), 0, 0, tiled=True)  30.4 us
    pallas_call x1, Pallas kernels, row_stage(): pl.pallas_call(row_kernel, out_shape=jax.ShapeDtypeStruct((groups, 2, num...  4.72 us
    pallas_call x1, Pallas kernels, column_stage(): pl.pallas_call(column_kernel, out_shape=jax.ShapeDtypeStruct((groups, 2,...  4.41 us
    pallas_call x1, Pallas kernels, final_stage(): pl.pallas_call(functools.partial(final_kernel, scale=scale), out_shape=ja...  3.45 us

profile of v13, /device:TPU:14, one launch (start us, length us, event | category | flops | bytes accessed | tf_op | source)
XLA Modules:
  0.0 100.4 jit_solution(1884334964029282415)
XLA Ops:
  0.0 4.7 %shard_map.109 = f32[16,2,6,16,128]{4,3,2,1,0:T(8,128)} custom-call(s32[6,512,128]{2,1,0:T(8,128)} %limbs_ref.1, bf16[1024,512]{1,0:T(8,128)(2,1)} %constant.20.clone.matrix_ref, f32[256,128]{1,0:T(8,128)} %constant.22.clone.base_cos_ref, f32[256,128]{1,0:T(8,128)} %constant.23.clone.base_sin_ref, f32[256,128]{1,0:T(8,128)} %constant.24.clone.lane_cos_ref, ...), custom_call_target="tpu_custom_call" | custom-call | flops 1610612736 | bytes 5767168 | tf_op jit(solution)/shard_map/pallas_call | solution.py:89
  4.7 57.4 %all_to_all.10.in_ref = f32[16,2,6,16,128]{4,3,2,1,0:T(8,128)} all-to-all(f32[16,2,6,16,128]{4,3,2,1,0:T(8,128)} %shard_map.109), channel_id=1, replica_groups=mesh['pair'=32,'row'=2,'col'=8] {'row','col'}, dimensions={0} | all-to-all | bytes 3145728 | tf_op jit(solution)/shard_map/all_to_all | solution.py:302
  62.1 4.4 %shard_map.110 = f32[16,2,3,16,128]{4,3,2,1,0:T(8,128)} custom-call(f32[16,2,6,16,128]{4,3,2,1,0:T(8,128)} %all_to_all.10.in_ref, f32[16,128]{1,0:T(8,128)} %constant.26.clone.twist_cos_ref, f32[16,128]{1,0:T(8,128)} %constant.27.clone.twist_sin_ref, bf16[512,256]{1,0:T(8,128)(2,1)} %constant.28.clone.forward_ref, bf16[512,256]{1,0:T(8,128)(2,1)} %constant.29.clone.inverse_ref), custom_call_target="tpu_custom_call" | custom-call | flops 905969664 | bytes 2359296 | tf_op jit(solution)/shard_map/pallas_call | solution.py:253
  66.5 30.4 %all_to_all.11.pieces_ref = f32[16,2,3,16,128]{4,3,2,1,0:T(8,128)} all-to-all(f32[16,2,3,16,128]{4,3,2,1,0:T(8,128)} %shard_map.110), channel_id=1, replica_groups=mesh['pair'=32,'row'=2,'col'=8] {'row','col'}, dimensions={0} | all-to-all | bytes 1572864 | tf_op jit(solution)/shard_map/all_to_all | solution.py:319
  96.9 3.5 %shard_map.111 = f32[3,512,128]{2,1,0:T(8,128)} custom-call(f32[16,2,3,16,128]{4,3,2,1,0:T(8,128)} %all_to_all.11.pieces_ref, bf16[1024,512]{1,0:T(8,128)(2,1)} %constant.21.clone.matrix_ref, f32[256,128]{1,0:T(8,128)} %constant.22.clone.base_cos_ref, f32[256,128]{1,0:T(8,128)} %constant.23.clone.base_sin_ref, f32[256,128]{1,0:T(8,128)} %constant.24.clone.lane_cos_ref, ...), custom_call_target="tpu_custom_call" | custom-call | flops 1207959552 | bytes 3407872 | tf_op jit(solution)/shard_map/pallas_call | solution.py:140

commit v14 on v13

--- a/solution.py
+++ b/solution.py
@@ -250,12 +250,19 @@
     groups, _, number, local, narrow = received.shape
     outputs = 3
     rows = groups * local
+    steps = 2
+    block = local // steps
+    fixed = lambda shape: pl.BlockSpec(shape, lambda s: (0,) * len(shape))
     return pl.pallas_call(
         column_kernel,
         out_shape=jax.ShapeDtypeStruct((groups, 2, outputs, local, narrow), jnp.float32),
+        grid=(steps,),
+        in_specs=[pl.BlockSpec((groups, 2, number, block, narrow), lambda s: (0, 0, 0, s, 0))]
+        + [fixed(table.shape) for table in (twist_cos, twist_sin, forward, inverse)],
+        out_specs=pl.BlockSpec((groups, 2, outputs, block, narrow), lambda s: (0, 0, 0, s, 0)),
         scratch_shapes=[
-            pltpu.VMEM((groups, number, local, 2 * narrow), jnp.float32),
-            pltpu.VMEM((groups, outputs, local, 2 * narrow), jnp.float32),
+            pltpu.VMEM((groups, number, block, 2 * narrow), jnp.float32),
+            pltpu.VMEM((groups, outputs, block, 2 * narrow), jnp.float32),
         ],
         cost_estimate=pl.CostEstimate(
             flops=3 * 2 * rows * (number + outputs) * (2 * narrow) ** 2,

time: 101 us -> 101 us (level)
  no operation moved by 1% of the time
where the time goes in v14:
time: 101 us; the launch traced here: 100 us
  blocking collectives  87.8 us (87%)
  Pallas kernels  12.4 us (12%)
    all_to_all x1, blocking collectives, body(): received = lax.all_to_all(send, ('row', 'col'), 0, 0, tiled=True)  57.4 us
    all_to_all x1, blocking collectives, body(): pieces = lax.all_to_all(outgoing, ('row', 'col'), 0, 0, tiled=True)  30.4 us
    pallas_call x1, Pallas kernels, row_stage(): pl.pallas_call(row_kernel, out_shape=jax.ShapeDtypeStruct((groups, 2, num...  4.72 us
    pallas_call x1, Pallas kernels, column_stage(): pl.pallas_call(column_kernel, out_shape=jax.ShapeDtypeStruct((groups, 2,...  4.25 us
    pallas_call x1, Pallas kernels, final_stage(): pl.pallas_call(functools.partial(final_kernel, scale=scale), out_shape=ja...  3.46 us

profile of v14, /device:TPU:14, one launch (start us, length us, event | category | flops | bytes accessed | tf_op | source)
XLA Modules:
  0.0 100.2 jit_solution(16803054502623860704)
XLA Ops:
  0.0 4.7 %shard_map.109 = f32[16,2,6,16,128]{4,3,2,1,0:T(8,128)} custom-call(s32[6,512,128]{2,1,0:T(8,128)} %limbs_ref.1, bf16[1024,512]{1,0:T(8,128)(2,1)} %constant.20.clone.matrix_ref, f32[256,128]{1,0:T(8,128)} %constant.22.clone.base_cos_ref, f32[256,128]{1,0:T(8,128)} %constant.23.clone.base_sin_ref, f32[256,128]{1,0:T(8,128)} %constant.24.clone.lane_cos_ref, ...), custom_call_target="tpu_custom_call" | custom-call | flops 1610612736 | bytes 5767168 | tf_op jit(solution)/shard_map/pallas_call | solution.py:89
  4.7 57.4 %all_to_all.10.in_ref = f32[16,2,6,16,128]{4,3,2,1,0:T(8,128)} all-to-all(f32[16,2,6,16,128]{4,3,2,1,0:T(8,128)} %shard_map.109), channel_id=1, replica_groups=mesh['pair'=32,'row'=2,'col'=8] {'row','col'}, dimensions={0} | all-to-all | bytes 3145728 | tf_op jit(solution)/shard_map/all_to_all | solution.py:309
  62.1 4.2 %shard_map.110 = f32[16,2,3,16,128]{4,3,2,1,0:T(8,128)} custom-call(f32[16,2,6,16,128]{4,3,2,1,0:T(8,128)} %all_to_all.10.in_ref, f32[16,128]{1,0:T(8,128)} %constant.26.clone.twist_cos_ref, f32[16,128]{1,0:T(8,128)} %constant.27.clone.twist_sin_ref, bf16[512,256]{1,0:T(8,128)(2,1)} %constant.28.clone.forward_ref, bf16[512,256]{1,0:T(8,128)(2,1)} %constant.29.clone.inverse_ref), custom_call_target="tpu_custom_call" | custom-call | flops 905969664 | bytes 2359296 | tf_op jit(solution)/shard_map/pallas_call | solution.py:256
  66.3 30.4 %all_to_all.11.pieces_ref = f32[16,2,3,16,128]{4,3,2,1,0:T(8,128)} all-to-all(f32[16,2,3,16,128]{4,3,2,1,0:T(8,128)} %shard_map.110), channel_id=1, replica_groups=mesh['pair'=32,'row'=2,'col'=8] {'row','col'}, dimensions={0} | all-to-all | bytes 1572864 | tf_op jit(solution)/shard_map/all_to_all | solution.py:326
  96.8 3.5 %shard_map.111 = f32[3,512,128]{2,1,0:T(8,128)} custom-call(f32[16,2,3,16,128]{4,3,2,1,0:T(8,128)} %all_to_all.11.pieces_ref, bf16[1024,512]{1,0:T(8,128)(2,1)} %constant.21.clone.matrix_ref, f32[256,128]{1,0:T(8,128)} %constant.22.clone.base_cos_ref, f32[256,128]{1,0:T(8,128)} %constant.23.clone.base_sin_ref, f32[256,128]{1,0:T(8,128)} %constant.24.clone.lane_cos_ref, ...), custom_call_target="tpu_custom_call" | custom-call | flops 1207959552 | bytes 3407872 | tf_op jit(solution)/shard_map/pallas_call | solution.py:140

commit v15 on v14

--- a/solution.py
+++ b/solution.py
@@ -101,33 +101,36 @@
     )(limbs, matrix, *tables)
 
 
-def final_kernel(pieces_ref, matrix_ref, base_cos_ref, base_sin_ref, lane_cos_ref, lane_sin_ref, out_ref, *, scale):
+def final_kernel(pieces_ref, leading_ref, trailing_ref, base_cos_ref, base_sin_ref, lane_cos_ref, lane_sin_ref, out_ref, data_ref, *, scale):
     groups, _, outputs, local, narrow = pieces_ref.shape
     half = groups * local
-    turn_cos, turn_sin = turn_tables(base_cos_ref, base_sin_ref, lane_cos_ref, lane_sin_ref)
-    turn_cos = turn_cos.reshape(groups, local, narrow)
-    turn_sin = turn_sin.reshape(groups, local, narrow)
-    columns = []
-    for i in range(outputs):
-        real = pieces_ref[:, 0, i]
-        imag = pieces_ref[:, 1, i]
-        untwisted = jnp.concatenate(
-            (
-                (real * turn_cos + imag * turn_sin).reshape(half, narrow),
-                (imag * turn_cos - real * turn_sin).reshape(half, narrow),
-            ),
-            axis=0,
-        )
-        columns.append(untwisted)
-    gathered = jnp.concatenate(columns, axis=1)
-    first = gathered.astype(jnp.bfloat16)
-    second = (gathered - first.astype(jnp.float32)).astype(jnp.bfloat16)
-    height = matrix_ref.shape[0] // 2
     width = outputs * narrow
-    leading = jnp.dot(
-        matrix_ref[:height], jnp.concatenate((first, second), axis=1), preferred_element_type=jnp.float32
-    )
-    trailing = jnp.dot(matrix_ref[height:], first, preferred_element_type=jnp.float32)
+
+    @pl.when(pl.program_id(0) == 0)
+    def _():
+        turn_cos, turn_sin = turn_tables(base_cos_ref, base_sin_ref, lane_cos_ref, lane_sin_ref)
+        turn_cos = turn_cos.reshape(groups, local, narrow)
+        turn_sin = turn_sin.reshape(groups, local, narrow)
+        columns = []
+        for i in range(outputs):
+            real = pieces_ref[:, 0, i]
+            imag = pieces_ref[:, 1, i]
+            untwisted = jnp.concatenate(
+                (
+                    (real * turn_cos + imag * turn_sin).reshape(half, narrow),
+                    (imag * turn_cos - real * turn_sin).reshape(half, narrow),
+                ),
+                axis=0,
+            )
+            columns.append(untwisted)
+        gathered = jnp.concatenate(columns, axis=1)
+        first = gathered.astype(jnp.bfloat16)
+        second = (gathered - first.astype(jnp.float32)).astype(jnp.bfloat16)
+        data_ref[...] = jnp.concatenate((first, second), axis=1)
+
+    data = data_ref[...]
+    leading = jnp.dot(leading_ref[...], data, preferred_element_type=jnp.float32)
+    trailing = jnp.dot(trailing_ref[...], data[:, :width], preferred_element_type=jnp.float32)
     small = trailing + leading[:, width:]
     total = (small + leading[:, :width]) * scale
     for i in range(outputs):
@@ -137,15 +140,28 @@
 def final_stage(pieces, matrix, tables, scale):
     groups, _, outputs, local, narrow = pieces.shape
     height = matrix.shape[0] // 2
+    steps = 2
+    block = height // steps
+    fixed = lambda shape: pl.BlockSpec(shape, lambda s: (0,) * len(shape))
     return pl.pallas_call(
         functools.partial(final_kernel, scale=scale),
         out_shape=jax.ShapeDtypeStruct((outputs, height, narrow), jnp.float32),
+        grid=(steps,),
+        in_specs=[
+            fixed(pieces.shape),
+            pl.BlockSpec((block, matrix.shape[1]), lambda s: (s, 0)),
+            pl.BlockSpec((block, matrix.shape[1]), lambda s: (s, 0)),
+        ]
+        + [fixed(table.shape) for table in tables],
+        out_specs=pl.BlockSpec((outputs, block, narrow), lambda s: (0, s, 0)),
+        scratch_shapes=[pltpu.VMEM((2 * groups * local, 2 * outputs * narrow), jnp.bfloat16)],
+        compiler_params=pltpu.CompilerParams(dimension_semantics=("arbitrary",)),
         cost_estimate=pl.CostEstimate(
             flops=2 * 3 * height * height * 2 * outputs * narrow,
             transcendentals=0,
             bytes_accessed=4 * 3 * outputs * height * narrow + 2 * 2 * height * height,
         ),
-    )(pieces, matrix, *tables)
+    )(pieces, matrix[:height], matrix[height:], *tables)
 
 
 def fft16(real, imag, sign):

time: 101 us -> 101 us (level)
  no operation moved by 1% of the time
where the time goes in v15:
time: 101 us; the launch traced here: 100 us
  blocking collectives  87.8 us (87%)
  Pallas kernels  12.5 us (12%)
    all_to_all x1, blocking collectives, body(): received = lax.all_to_all(send, ('row', 'col'), 0, 0, tiled=True)  57.4 us
    all_to_all x1, blocking collectives, body(): pieces = lax.all_to_all(outgoing, ('row', 'col'), 0, 0, tiled=True)  30.4 us
    pallas_call x1, Pallas kernels, row_stage(): pl.pallas_call(row_kernel, out_shape=jax.ShapeDtypeStruct((groups, 2, num...  4.72 us
    pallas_call x1, Pallas kernels, column_stage(): pl.pallas_call(column_kernel, out_shape=jax.ShapeDtypeStruct((groups, 2,...  4.25 us
    pallas_call x1, Pallas kernels, final_stage(): pl.pallas_call(functools.partial(final_kernel, scale=scale), out_shape=ja...  3.54 us

profile of v15, /device:TPU:14, one launch (start us, length us, event | category | flops | bytes accessed | tf_op | source)
XLA Modules:
  0.0 100.3 jit_solution(17492096193862372857)
XLA Ops:
  0.0 4.7 %shard_map.109 = f32[16,2,6,16,128]{4,3,2,1,0:T(8,128)} custom-call(s32[6,512,128]{2,1,0:T(8,128)} %limbs_ref.1, bf16[1024,512]{1,0:T(8,128)(2,1)} %constant.20.clone.matrix_ref, f32[256,128]{1,0:T(8,128)} %constant.22.clone.base_cos_ref, f32[256,128]{1,0:T(8,128)} %constant.23.clone.base_sin_ref, f32[256,128]{1,0:T(8,128)} %constant.24.clone.lane_cos_ref, ...), custom_call_target="tpu_custom_call" | custom-call | flops 1610612736 | bytes 5767168 | tf_op jit(solution)/shard_map/pallas_call | solution.py:89
  4.7 57.4 %all_to_all.10.in_ref = f32[16,2,6,16,128]{4,3,2,1,0:T(8,128)} all-to-all(f32[16,2,6,16,128]{4,3,2,1,0:T(8,128)} %shard_map.109), channel_id=1, replica_groups=mesh['pair'=32,'row'=2,'col'=8] {'row','col'}, dimensions={0} | all-to-all | bytes 3145728 | tf_op jit(solution)/shard_map/all_to_all | solution.py:325
  62.1 4.2 %shard_map.110 = f32[16,2,3,16,128]{4,3,2,1,0:T(8,128)} custom-call(f32[16,2,6,16,128]{4,3,2,1,0:T(8,128)} %all_to_all.10.in_ref, f32[16,128]{1,0:T(8,128)} %constant.26.clone.twist_cos_ref, f32[16,128]{1,0:T(8,128)} %constant.27.clone.twist_sin_ref, bf16[512,256]{1,0:T(8,128)(2,1)} %constant.28.clone.forward_ref, bf16[512,256]{1,0:T(8,128)(2,1)} %constant.29.clone.inverse_ref), custom_call_target="tpu_custom_call" | custom-call | flops 905969664 | bytes 2359296 | tf_op jit(solution)/shard_map/pallas_call | solution.py:272
  66.3 30.4 %all_to_all.11.pieces_ref = f32[16,2,3,16,128]{4,3,2,1,0:T(8,128)} all-to-all(f32[16,2,3,16,128]{4,3,2,1,0:T(8,128)} %shard_map.110), channel_id=1, replica_groups=mesh['pair'=32,'row'=2,'col'=8] {'row','col'}, dimensions={0} | all-to-all | bytes 1572864 | tf_op jit(solution)/shard_map/all_to_all | solution.py:342
  96.8 3.5 %shard_map.111 = f32[3,512,128]{2,1,0:T(8,128)} custom-call(f32[16,2,3,16,128]{4,3,2,1,0:T(8,128)} %all_to_all.11.pieces_ref, bf16[512,512]{1,0:T(8,128)(2,1)} %constant.30.leading_ref, bf16[512,512]{1,0:T(8,128)(2,1)} %constant.31.trailing_ref, f32[256,128]{1,0:T(8,128)} %constant.22.clone.base_cos_ref, f32[256,128]{1,0:T(8,128)} %constant.23.clone.base_sin_ref, ...), custom_call_target="tpu_custom_call" | custom-call | flops 1207959552 | bytes 3407872 | tf_op jit(solution)/shard_map/pallas_call | solution.py:146

commit v16 on v14

--- a/solution.py
+++ b/solution.py
@@ -187,9 +187,8 @@
     first = values.astype(jnp.bfloat16)
     second = (values - first.astype(jnp.float32)).astype(jnp.bfloat16)
     major = matrix_ref[:size]
-    minor = matrix_ref[size:]
-    small = jnp.dot(second, major, preferred_element_type=jnp.float32) + jnp.dot(
-        first, minor, preferred_element_type=jnp.float32
+    small = jnp.dot(
+        jnp.concatenate((second, first), axis=1), matrix_ref[...], preferred_element_type=jnp.float32
     )
     return small + jnp.dot(first, major, preferred_element_type=jnp.float32)
 

time: 101 us -> 101 us (level)
  no operation moved by 1% of the time
where the time goes in v16:
time: 101 us; the launch traced here: 100 us
  blocking collectives  87.8 us (87%)
  Pallas kernels  12.4 us (12%)
    all_to_all x1, blocking collectives, body(): received = lax.all_to_all(send, ('row', 'col'), 0, 0, tiled=True)  57.4 us
    all_to_all x1, blocking collectives, body(): pieces = lax.all_to_all(outgoing, ('row', 'col'), 0, 0, tiled=True)  30.4 us
    pallas_call x1, Pallas kernels, row_stage(): pl.pallas_call(row_kernel, out_shape=jax.ShapeDtypeStruct((groups, 2, num...  4.72 us
    pallas_call x1, Pallas kernels, column_stage(): pl.pallas_call(column_kernel, out_shape=jax.ShapeDtypeStruct((groups, 2,...  4.25 us
    pallas_call x1, Pallas kernels, final_stage(): pl.pallas_call(functools.partial(final_kernel, scale=scale), out_shape=ja...  3.46 us

profile of v16, /device:TPU:14, one launch (start us, length us, event | category | flops | bytes accessed | tf_op | source)
XLA Modules:
  0.0 100.2 jit_solution(7888484735558373136)
XLA Ops:
  0.0 4.7 %shard_map.109 = f32[16,2,6,16,128]{4,3,2,1,0:T(8,128)} custom-call(s32[6,512,128]{2,1,0:T(8,128)} %limbs_ref.1, bf16[1024,512]{1,0:T(8,128)(2,1)} %constant.20.clone.matrix_ref, f32[256,128]{1,0:T(8,128)} %constant.22.clone.base_cos_ref, f32[256,128]{1,0:T(8,128)} %constant.23.clone.base_sin_ref, f32[256,128]{1,0:T(8,128)} %constant.24.clone.lane_cos_ref, ...), custom_call_target="tpu_custom_call" | custom-call | flops 1610612736 | bytes 5767168 | tf_op jit(solution)/shard_map/pallas_call | solution.py:89
  4.7 57.4 %all_to_all.10.in_ref = f32[16,2,6,16,128]{4,3,2,1,0:T(8,128)} all-to-all(f32[16,2,6,16,128]{4,3,2,1,0:T(8,128)} %shard_map.109), channel_id=1, replica_groups=mesh['pair'=32,'row'=2,'col'=8] {'row','col'}, dimensions={0} | all-to-all | bytes 3145728 | tf_op jit(solution)/shard_map/all_to_all | solution.py:308
  62.1 4.2 %shard_map.110 = f32[16,2,3,16,128]{4,3,2,1,0:T(8,128)} custom-call(f32[16,2,6,16,128]{4,3,2,1,0:T(8,128)} %all_to_all.10.in_ref, f32[16,128]{1,0:T(8,128)} %constant.26.clone.twist_cos_ref, f32[16,128]{1,0:T(8,128)} %constant.27.clone.twist_sin_ref, bf16[512,256]{1,0:T(8,128)(2,1)} %constant.28.clone.forward_ref, bf16[512,256]{1,0:T(8,128)(2,1)} %constant.29.clone.inverse_ref), custom_call_target="tpu_custom_call" | custom-call | flops 905969664 | bytes 2359296 | tf_op jit(solution)/shard_map/pallas_call | solution.py:255
  66.3 30.4 %all_to_all.11.pieces_ref = f32[16,2,3,16,128]{4,3,2,1,0:T(8,128)} all-to-all(f32[16,2,3,16,128]{4,3,2,1,0:T(8,128)} %shard_map.110), channel_id=1, replica_groups=mesh['pair'=32,'row'=2,'col'=8] {'row','col'}, dimensions={0} | all-to-all | bytes 1572864 | tf_op jit(solution)/shard_map/all_to_all | solution.py:325
  96.8 3.5 %shard_map.111 = f32[3,512,128]{2,1,0:T(8,128)} custom-call(f32[16,2,3,16,128]{4,3,2,1,0:T(8,128)} %all_to_all.11.pieces_ref, bf16[1024,512]{1,0:T(8,128)(2,1)} %constant.21.clone.matrix_ref, f32[256,128]{1,0:T(8,128)} %constant.22.clone.base_cos_ref, f32[256,128]{1,0:T(8,128)} %constant.23.clone.base_sin_ref, f32[256,128]{1,0:T(8,128)} %constant.24.clone.lane_cos_ref, ...), custom_call_target="tpu_custom_call" | custom-call | flops 1207959552 | bytes 3407872 | tf_op jit(solution)/shard_map/pallas_call | solution.py:140

commit v17 on v16

--- a/solution.py
+++ b/solution.py
@@ -55,13 +55,14 @@
     centred = [limbs_ref[i] - jnp.int32(32768) for i in range(number)]
     upper = [lax.shift_right_arithmetic(value, jnp.int32(8)) for value in centred]
     lower = [value - top * jnp.int32(256) for value, top in zip(centred, upper)]
+    upper = [value - low for value, low in zip(centred, lower)]
     pieces = jnp.concatenate(upper + lower, axis=1).astype(jnp.float32).astype(jnp.bfloat16)
     products = jnp.dot(matrix_ref[...], pieces, preferred_element_type=jnp.float32)
     count = 2 * half
     width = number * narrow
     upper_part = products[:count, :width] + products[count:, :width]
     lower_part = products[:count, width:] + products[count:, width:]
-    rows = (upper_part * 256.0 + lower_part) * (1.0 / 32768.0)
+    rows = upper_part + lower_part
     for i in range(number):
         real_rows = rows[:half, i * narrow : (i + 1) * narrow]
         imag_rows = rows[half:, i * narrow : (i + 1) * narrow]
@@ -285,7 +286,7 @@
     row_cos_exact, row_sin_exact = exact_phases(
         row_index[None, :] * (2 * half_index[:, None] + 1) % (2 * height), height
     )
-    row_matrix = jnp.asarray(split_bf16(np.concatenate((row_cos_exact, row_sin_exact), axis=0)))
+    row_matrix = jnp.asarray(split_bf16(np.concatenate((row_cos_exact, row_sin_exact), axis=0) / 32768.0))
     final_matrix = jnp.asarray(split_bf16(np.concatenate((row_cos_exact, row_sin_exact), axis=0).T))
     device_index = np.arange(groups, dtype=np.int64)
     base_cos, base_sin = exact_phases(

time: 101 us -> 100 us (0.990)
  the two profiles are of different devices: /device:TPU:14 before, /device:TPU:12 now
where the time goes in v17:
time: 100 us
  blocking collectives  87.7 us (88%)
  Pallas kernels  12.4 us (12%)
    all_to_all x1, blocking collectives, body(): received = lax.all_to_all(send, ('row', 'col'), 0, 0, tiled=True)  57.3 us
    all_to_all x1, blocking collectives, body(): pieces = lax.all_to_all(outgoing, ('row', 'col'), 0, 0, tiled=True)  30.4 us
    pallas_call x1, Pallas kernels, row_stage(): pl.pallas_call(row_kernel, out_shape=jax.ShapeDtypeStruct((groups, 2, num...  4.69 us
    pallas_call x1, Pallas kernels, column_stage(): pl.pallas_call(column_kernel, out_shape=jax.ShapeDtypeStruct((groups, 2,...  4.25 us
    pallas_call x1, Pallas kernels, final_stage(): pl.pallas_call(functools.partial(final_kernel, scale=scale), out_shape=ja...  3.46 us

profile of v17, /device:TPU:12, one launch (start us, length us, event | category | flops | bytes accessed | tf_op | source)
XLA Modules:
  0.0 100.1 jit_solution(14937145689149148822)
XLA Ops:
  0.0 4.7 %shard_map.109 = f32[16,2,6,16,128]{4,3,2,1,0:T(8,128)} custom-call(s32[6,512,128]{2,1,0:T(8,128)} %limbs_ref.1, bf16[1024,512]{1,0:T(8,128)(2,1)} %constant.20.clone.matrix_ref, f32[256,128]{1,0:T(8,128)} %constant.22.clone.base_cos_ref, f32[256,128]{1,0:T(8,128)} %constant.23.clone.base_sin_ref, f32[256,128]{1,0:T(8,128)} %constant.24.clone.lane_cos_ref, ...), custom_call_target="tpu_custom_call" | custom-call | flops 1610612736 | bytes 5767168 | tf_op jit(solution)/shard_map/pallas_call | solution.py:90
  4.7 57.3 %all_to_all.10.in_ref = f32[16,2,6,16,128]{4,3,2,1,0:T(8,128)} all-to-all(f32[16,2,6,16,128]{4,3,2,1,0:T(8,128)} %shard_map.109), channel_id=1, replica_groups=mesh['pair'=32,'row'=2,'col'=8] {'row','col'}, dimensions={0} | all-to-all | bytes 3145728 | tf_op jit(solution)/shard_map/all_to_all | solution.py:309
  62.0 4.2 %shard_map.110 = f32[16,2,3,16,128]{4,3,2,1,0:T(8,128)} custom-call(f32[16,2,6,16,128]{4,3,2,1,0:T(8,128)} %all_to_all.10.in_ref, f32[16,128]{1,0:T(8,128)} %constant.26.clone.twist_cos_ref, f32[16,128]{1,0:T(8,128)} %constant.27.clone.twist_sin_ref, bf16[512,256]{1,0:T(8,128)(2,1)} %constant.28.clone.forward_ref, bf16[512,256]{1,0:T(8,128)(2,1)} %constant.29.clone.inverse_ref), custom_call_target="tpu_custom_call" | custom-call | flops 905969664 | bytes 2359296 | tf_op jit(solution)/shard_map/pallas_call | solution.py:256
  66.3 30.4 %all_to_all.11.pieces_ref = f32[16,2,3,16,128]{4,3,2,1,0:T(8,128)} all-to-all(f32[16,2,3,16,128]{4,3,2,1,0:T(8,128)} %shard_map.110), channel_id=1, replica_groups=mesh['pair'=32,'row'=2,'col'=8] {'row','col'}, dimensions={0} | all-to-all | bytes 1572864 | tf_op jit(solution)/shard_map/all_to_all | solution.py:326
  96.6 3.5 %shard_map.111 = f32[3,512,128]{2,1,0:T(8,128)} custom-call(f32[16,2,3,16,128]{4,3,2,1,0:T(8,128)} %all_to_all.11.pieces_ref, bf16[1024,512]{1,0:T(8,128)(2,1)} %constant.21.clone.matrix_ref, f32[256,128]{1,0:T(8,128)} %constant.22.clone.base_cos_ref, f32[256,128]{1,0:T(8,128)} %constant.23.clone.base_sin_ref, f32[256,128]{1,0:T(8,128)} %constant.24.clone.lane_cos_ref, ...), custom_call_target="tpu_custom_call" | custom-call | flops 1207959552 | bytes 3407872 | tf_op jit(solution)/shard_map/pallas_call | solution.py:141

commit v18 on v17

--- a/solution.py
+++ b/solution.py
@@ -130,7 +130,7 @@
     )
     trailing = jnp.dot(matrix_ref[height:], first, preferred_element_type=jnp.float32)
     small = trailing + leading[:, width:]
-    total = (small + leading[:, :width]) * scale
+    total = small + leading[:, :width]
     for i in range(outputs):
         out_ref[i] = total[:, i * narrow : (i + 1) * narrow]
 
@@ -287,7 +287,9 @@
         row_index[None, :] * (2 * half_index[:, None] + 1) % (2 * height), height
     )
     row_matrix = jnp.asarray(split_bf16(np.concatenate((row_cos_exact, row_sin_exact), axis=0) / 32768.0))
-    final_matrix = jnp.asarray(split_bf16(np.concatenate((row_cos_exact, row_sin_exact), axis=0).T))
+    final_matrix = jnp.asarray(
+        split_bf16(np.concatenate((row_cos_exact, row_sin_exact), axis=0).T * (2.0 / (limb_total * math.sqrt(limb_total))))
+    )
     device_index = np.arange(groups, dtype=np.int64)
     base_cos, base_sin = exact_phases(
         device_index[:, None] * narrow * (2 * half_index[None, :] + 1), limb_total

time: 100 us -> 100 us (level)
  the two profiles are of different devices: /device:TPU:12 before, /device:TPU:14 now
where the time goes in v18:
time: 100 us
  blocking collectives  87.7 us (88%)
  Pallas kernels  12.4 us (12%)
    all_to_all x1, blocking collectives, body(): received = lax.all_to_all(send, ('row', 'col'), 0, 0, tiled=True)  57.3 us
    all_to_all x1, blocking collectives, body(): pieces = lax.all_to_all(outgoing, ('row', 'col'), 0, 0, tiled=True)  30.4 us
    pallas_call x1, Pallas kernels, row_stage(): pl.pallas_call(row_kernel, out_shape=jax.ShapeDtypeStruct((groups, 2, num...  4.68 us
    pallas_call x1, Pallas kernels, column_stage(): pl.pallas_call(column_kernel, out_shape=jax.ShapeDtypeStruct((groups, 2,...  4.25 us
    pallas_call x1, Pallas kernels, final_stage(): pl.pallas_call(functools.partial(final_kernel, scale=scale), out_shape=ja...  3.45 us

profile of v18, /device:TPU:14, one launch (start us, length us, event | category | flops | bytes accessed | tf_op | source)
XLA Modules:
  0.0 100.1 jit_solution(15905839283553260630)
XLA Ops:
  0.0 4.7 %shard_map.109 = f32[16,2,6,16,128]{4,3,2,1,0:T(8,128)} custom-call(s32[6,512,128]{2,1,0:T(8,128)} %limbs_ref.1, bf16[1024,512]{1,0:T(8,128)(2,1)} %constant.20.clone.matrix_ref, f32[256,128]{1,0:T(8,128)} %constant.22.clone.base_cos_ref, f32[256,128]{1,0:T(8,128)} %constant.23.clone.base_sin_ref, f32[256,128]{1,0:T(8,128)} %constant.24.clone.lane_cos_ref, ...), custom_call_target="tpu_custom_call" | custom-call | flops 1610612736 | bytes 5767168 | tf_op jit(solution)/shard_map/pallas_call | solution.py:90
  4.7 57.3 %all_to_all.10.in_ref = f32[16,2,6,16,128]{4,3,2,1,0:T(8,128)} all-to-all(f32[16,2,6,16,128]{4,3,2,1,0:T(8,128)} %shard_map.109), channel_id=1, replica_groups=mesh['pair'=32,'row'=2,'col'=8] {'row','col'}, dimensions={0} | all-to-all | bytes 3145728 | tf_op jit(solution)/shard_map/all_to_all | solution.py:311
  62.0 4.2 %shard_map.110 = f32[16,2,3,16,128]{4,3,2,1,0:T(8,128)} custom-call(f32[16,2,6,16,128]{4,3,2,1,0:T(8,128)} %all_to_all.10.in_ref, f32[16,128]{1,0:T(8,128)} %constant.26.clone.twist_cos_ref, f32[16,128]{1,0:T(8,128)} %constant.27.clone.twist_sin_ref, bf16[512,256]{1,0:T(8,128)(2,1)} %constant.28.clone.forward_ref, bf16[512,256]{1,0:T(8,128)(2,1)} %constant.29.clone.inverse_ref), custom_call_target="tpu_custom_call" | custom-call | flops 905969664 | bytes 2359296 | tf_op jit(solution)/shard_map/pallas_call | solution.py:256
  66.3 30.4 %all_to_all.11.pieces_ref = f32[16,2,3,16,128]{4,3,2,1,0:T(8,128)} all-to-all(f32[16,2,3,16,128]{4,3,2,1,0:T(8,128)} %shard_map.110), channel_id=1, replica_groups=mesh['pair'=32,'row'=2,'col'=8] {'row','col'}, dimensions={0} | all-to-all | bytes 1572864 | tf_op jit(solution)/shard_map/all_to_all | solution.py:328
  96.6 3.5 %shard_map.111 = f32[3,512,128]{2,1,0:T(8,128)} custom-call(f32[16,2,3,16,128]{4,3,2,1,0:T(8,128)} %all_to_all.11.pieces_ref, bf16[1024,512]{1,0:T(8,128)(2,1)} %constant.21.clone.matrix_ref, f32[256,128]{1,0:T(8,128)} %constant.22.clone.base_cos_ref, f32[256,128]{1,0:T(8,128)} %constant.23.clone.base_sin_ref, f32[256,128]{1,0:T(8,128)} %constant.24.clone.lane_cos_ref, ...), custom_call_target="tpu_custom_call" | custom-call | flops 1207959552 | bytes 3407872 | tf_op jit(solution)/shard_map/pallas_call | solution.py:141
